TPU v7x, 256 devices: a whole 4x4x8 slice. The times are simulated.
256 devices in a mesh: clip: 8 (over x_hi, y), feat: 32 (over z, x_lo, core).
Axes of the slice: x: 4 (x_hi: 2, x_lo: 2; x = x_hi * 2 + x_lo), y: 4, z: 8, core: 2. Of those that a mesh axis runs over, the one named last changes fastest.
Arguments:
- embeds: float32 [8192, 1152], P('clip', 'feat'), may hold values from -6 to 6
- frequencies: float32 [1152, 20480], P('clip', 'feat'), may hold values from -0.5 to 0.5
- phases: float32 [20480], P('feat'), may hold values from -3.140625 to 3.140625
- weights: float32 [20480, 128], P('feat', 'clip'), may hold values from -6 to 6
- labels: int32 [8192, 128], P('clip'), may hold values 0 or 1
Outputs:
- trained: float32 [20480, 128], P('feat', 'clip')
- scores: float32 [8192, 128], P('clip', 'feat')
All inputs are finite; a program needn't handle non-finite values. No bound on the sum of `labels` on one device may be relied on, other than what follows from the above.
Results may differ from a plain program's by a relative error of at most 0.0055.
Values may be sent and summed in bfloat16 or wider, within the bound.
A program may use at most 64 MiB of HBM per device.

v0:
```python
import math

import jax
import jax.numpy as jnp
from jax import lax
from jax.sharding import PartitionSpec as P

STEPS = 2


def summed_logits(partial_value):
    return lax.psum(partial_value, "feat")


def per_device(embeds, frequencies, phases, weights, labels):
    freq_full = lax.all_gather(frequencies, "clip", axis=0, tiled=True)
    feat_count = frequencies.shape[1]
    total_features = feat_count * lax.axis_size("feat")
    out_width = weights.shape[1] * lax.axis_size("clip")
    share_width = out_width // lax.axis_size("feat")
    angles = jnp.dot(
        lax.all_gather(embeds, "feat", axis=1, tiled=True),
        freq_full,
        precision=lax.Precision.HIGHEST,
        preferred_element_type=jnp.float32,
    )
    feature_scale = math.sqrt(2.0 / total_features)
    phi = (feature_scale * jnp.cos(angles + phases[None, :])).astype(jnp.bfloat16)
    full_weights = lax.all_gather(weights, "clip", axis=1, tiled=True)
    own_weights = weights
    weight_half = full_weights.astype(jnp.bfloat16)
    targets = labels.astype(jnp.float32)
    feat_start = lax.axis_index("feat") * share_width
    for step in range(STEPS):
        partial_value = jnp.dot(phi, weight_half, preferred_element_type=jnp.float32)
        summed = summed_logits(partial_value)
        residual = (jax.nn.sigmoid(summed) - targets).astype(jnp.bfloat16)
        grad_part = lax.dot_general(
            phi, residual, (((0,), (0,)), ((), ())), preferred_element_type=jnp.float32
        )
        grad_own = lax.psum_scatter(grad_part, "clip", scatter_dimension=1, tiled=True)
        own_weights = own_weights - 0.25 * grad_own
        weight_half = lax.all_gather(own_weights.astype(jnp.bfloat16), "clip", axis=1, tiled=True)
    partial_value = jnp.dot(phi, weight_half, preferred_element_type=jnp.float32)
    summed = summed_logits(partial_value)
    scores = lax.dynamic_slice_in_dim(summed, feat_start, share_width, 1)
    return (own_weights, scores)


def solution(mesh):
    placed = (P("clip", "feat"), P("clip", "feat"), P("feat"), P("feat", "clip"), P("clip", None))
    return jax.shard_map(
        per_device,
        mesh=mesh,
        in_specs=placed,
        out_specs=(P("feat", "clip"), P("clip", "feat")),
        check_vma=False,
    )
```

profile of v0, /device:TPU:1, one launch (start us, length us, event | category | flops | bytes accessed | tf_op | source)
XLA Modules:
  0.0 1094.3 jit_solution(6680869996846778569)
XLA Ops:
  7.2 0.0 all-gather.6.cloned.1.call-start
  7.2 0.7 all-gather.6.cloned.1.call-update
  7.9 0.0 all-gather.4.cloned.1.call-start
  7.9 0.7 all-gather.4.cloned.1.call-update
  8.6 0.0 all-reduce.4.cloned.1.call-start
  8.7 0.8 convert
  9.5 29.4 %all_gather.17 = bf16[640,128]{0,1:T(8,128)(2,1)S(1)} all-gather(bf16[640,16]{0,1:T(8,128)(2,1)S(1)} %convert), channel_id=1, replica_groups=mesh['clip'=8,'feat'=32] {'clip'}, dimensions={1}, use_global_device_ids=true | all-gather | bytes 184320 | tf_op jit(solution)/shard_map/all_gather | solution.py:29
  38.8 0.0 copy-start.3
  38.8 43.2 %all-gather.6.cloned.1.call-done = f32[32,36,1024]{2,1,0:T(8,128)} async-done(((f32[1,36,1024]{2,1,0:T(8,128)}), f32[32,36,1024]{2,1,0:T(8,128)}) %all-gather.6.cloned.1.call-update) | async-done | bytes 4718608 | tf_op jit(solution)/shard_map/all_gather | solution.py:22
  82.0 5.2 reshape.6
  87.3 61.4 %all-gather.4.cloned.1.call-done = f32[1152,640]{1,0:T(8,128)} async-done(((f32[144,640]{1,0:T(8,128)}), f32[1152,640]{1,0:T(8,128)}) %all-gather.4.cloned.1.call-update) | async-done | bytes 2949136 | tf_op jit(solution)/shard_map/all_gather | solution.py:16
  148.6 0.0 copy-done.3
  148.6 23.3 %multiply_convert_fusion = bf16[1024,640]{1,0:T(8,128)(2,1)S(1)} fusion(f32[1152,1024]{1,0:T(8,128)} %reshape.6, f32[1152,640]{1,0:T(8,128)} %all-gather.4.cloned.1.call-done, f32[640]{0:T(1024)S(1)} %copy-done.3), kind=kOutput, calls=%fused_computation | convolution fusion | flops 9061662720 | bytes 8980992 | tf_op jit(solution)/shard_map/dot_general | solution.py:21
  172.0 0.0 copy-start.2
  172.0 1.3 fusion.12
  173.3 0.0 all-reduce.4.cloned.1.call-update
  173.3 0.0 copy-start
  173.3 0.0 reduce-scatter.3.cloned.1.call-start
  173.4 226.3 %all-reduce.4.cloned.1.call-done = f32[1024,128]{1,0:T(8,128)} async-done(((f32[1024,128]{1,0:T(8,128)}), f32[1024,128]{1,0:T(8,128)}) %all-reduce.4.cloned.1.call-update) | async-done | bytes 524304 | tf_op jit(solution)/shard_map/psum | solution.py:12
  399.6 0.0 copy-done.2
  399.6 2.2 fusion
  401.8 0.0 reduce-scatter.3.cloned.1.call-update
  401.9 0.0 all-reduce.6.cloned.1.call-start
  401.9 75.8 %reduce-scatter.3.cloned.1.call-done = f32[640,16]{0,1:T(8,128)} async-done(((f32[640,128]{0,1:T(8,128)}), f32[640,16]{0,1:T(8,128)}) %reduce-scatter.3.cloned.1.call-update) | async-done | bytes 40976 | tf_op jit(solution)/shard_map/reduce_scatter | solution.py:41
  477.7 0.0 copy-done
  477.7 0.8 fusion.6
  478.5 27.9 %all_gather.18 = bf16[640,128]{0,1:T(8,128)(2,1)S(1)} all-gather(bf16[640,16]{0,1:T(8,128)(2,1)S(1)} %fusion.6), channel_id=1, replica_groups=mesh['clip'=8,'feat'=32] {'clip'}, dimensions={1}, use_global_device_ids=true | all-gather | bytes 184320 | tf_op jit(solution)/shard_map/all_gather | solution.py:43
  506.4 1.3 fusion.10
  507.7 0.0 all-reduce.6.cloned.1.call-update
  507.7 0.0 copy-start.1
  507.7 0.0 reduce-scatter.5.cloned.1.call-start
  507.7 234.8 %all-reduce.6.cloned.1.call-done = f32[1024,128]{1,0:T(8,128)} async-done(((f32[1024,128]{1,0:T(8,128)}), f32[1024,128]{1,0:T(8,128)}) %all-reduce.6.cloned.1.call-update) | async-done | bytes 524304 | tf_op jit(solution)/shard_map/psum | solution.py:12
  742.5 2.2 fusion.1
  744.8 0.0 reduce-scatter.5.cloned.1.call-update
  744.8 0.0 all-reduce.8.cloned.1.call-start
  744.8 75.8 %reduce-scatter.5.cloned.1.call-done = f32[640,16]{0,1:T(8,128)} async-done(((f32[640,128]{0,1:T(8,128)}), f32[640,16]{0,1:T(8,128)}) %reduce-scatter.5.cloned.1.call-update) | async-done | bytes 40976 | tf_op jit(solution)/shard_map/reduce_scatter | solution.py:41
  820.6 0.0 copy-done.1
  820.6 1.4 fusion.9
  822.0 27.9 %all_gather.19 = bf16[640,128]{0,1:T(8,128)(2,1)S(1)} all-gather(bf16[640,16]{0,1:T(8,128)(2,1)S(1)} %get-tuple-element.2), channel_id=1, replica_groups=mesh['clip'=8,'feat'=32] {'clip'}, dimensions={1}, use_global_device_ids=true | all-gather | bytes 184320 | tf_op jit(solution)/shard_map/all_gather | solution.py:43
  849.9 1.3 fusion.11
  851.2 0.0 all-reduce.8.cloned.1.call-update
  851.3 234.8 %all-reduce.8.cloned.1.call-done = f32[1024,128]{0,1:T(8,128)} async-done(((f32[1024,128]{0,1:T(8,128)}), f32[1024,128]{0,1:T(8,128)}) %all-reduce.8.cloned.1.call-update) | async-done | bytes 524304 | tf_op jit(solution)/shard_map/psum | solution.py:12
  1086.1 1.4 constant_dynamic-slice_fusion
Async XLA Ops:
  7.2 74.9 %all-gather.6.cloned.1.call-start = ((), (), s32[]{:S(2)}) async-start(), calls=%async_computation.8 | async-start | bytes 5406720 | tf_op jit(solution)/shard_map/all_gather | solution.py:22
  7.9 140.7 %all-gather.4.cloned.1.call-start = ((), (), s32[]{:S(2)}) async-start(), calls=%async_computation.2 | async-start | bytes 3317760 | tf_op jit(solution)/shard_map/all_gather | solution.py:16
  8.6 391.0 %all-reduce.4.cloned.1.call-start = ((), (), s32[]{:S(2)}) async-start(), calls=%async_computation.3 | async-start | bytes 1048576 | tf_op jit(solution)/shard_map/psum | solution.py:12
  38.8 109.8 %copy-start.3 = (f32[640]{0:T(1024)S(1)}, f32[640]{0:T(1024)}, u32[]{:S(2)}) copy-start(f32[640]{0:T(1024)} %param.7) | copy-start | bytes 7684
  172.0 227.6 %copy-start.2 = (s32[1024,128]{1,0:T(8,128)S(1)}, s32[1024,128]{1,0:T(8,128)}, u32[]{:S(2)}) copy-start(s32[1024,128]{1,0:T(8,128)} %param.9) | copy-start | bytes 1572868
  173.3 304.4 %copy-start = (f32[640,16]{0,1:T(8,128)S(1)}, f32[640,16]{0,1:T(8,128)}, u32[]{:S(2)}) copy-start(f32[640,16]{0,1:T(8,128)} %param.8) | copy-start | bytes 122884
  173.3 304.4 %reduce-scatter.3.cloned.1.call-start = ((), (), s32[]{:S(2)}) async-start(), calls=%async_computation.4 | async-start | bytes 368640 | tf_op jit(solution)/shard_map/reduce_scatter | solution.py:41
  401.9 340.7 %all-reduce.6.cloned.1.call-start = ((), (), s32[]{:S(2)}) async-start(), calls=%async_computation.5 | async-start | bytes 1048576 | tf_op jit(solution)/shard_map/psum | solution.py:12
  507.7 313.0 %copy-start.1 = (f32[640,16]{0,1:T(8,128)S(1)}, f32[640,16]{0,1:T(8,128)}, u32[]{:S(2)}) copy-start(f32[640,16]{0,1:T(8,128)} %reduce-scatter.3.cloned.1.call-done) | copy-start | bytes 122884
  507.7 312.9 %reduce-scatter.5.cloned.1.call-start = ((), (), s32[]{:S(2)}) async-start(), calls=%async_computation.6 | async-start | bytes 368640 | tf_op jit(solution)/shard_map/reduce_scatter | solution.py:41
  744.8 341.3 %all-reduce.8.cloned.1.call-start = ((), (), s32[]{:S(2)}) async-start(), calls=%async_computation.7 | async-start | bytes 1048576 | tf_op jit(solution)/shard_map/psum | solution.py:12
Sparse Core Ops, SparseCore 0:
  9.8 72.1 all-gather.5
  84.6 63.9 all-gather.3
  173.4 226.1 all-reduce.3
  403.3 74.3 reduce-scatter.2
  507.8 234.6 all-reduce.5
  746.2 74.3 reduce-scatter.4
  851.4 234.6 all-reduce.7
where the time goes:
time: 1090 us
  waiting for transfers between devices  954 us (88%)
  blocking collectives  85.1 us (8%)
  matrix products  31.7 us (3%)
  between operations  14.2 us (1%)
    psum x3, waiting for transfers between devices, summed_logits(): return lax.psum(partial_value, 'feat')  696 us
    reduce_scatter x2, waiting for transfers between devices, per_device(): lax.psum_scatter(grad_part, 'clip', scatter_dimension=1, tiled=True)  152 us
    all_gather x1, waiting for transfers between devices, per_device(): freq_full = lax.all_gather(frequencies, 'clip', axis=0, tiled=True)  61.4 us
    all_gather x2, blocking collectives, per_device(): lax.all_gather(own_weights.astype(jnp.bfloat16), 'clip', axis=1, tiled=True)  55.7 us
    all_gather x1, waiting for transfers between devices, per_device(): lax.all_gather(embeds, 'feat', axis=1, tiled=True)  43.2 us
    all_gather x1, blocking collectives, per_device(): full_weights = lax.all_gather(weights, 'clip', axis=1, tiled=True)  29.4 us
    dot_general x1, matrix products, per_device(): jnp.dot(lax.all_gather(embeds, 'feat', axis=1, tiled=True), freq_full, pr...  23.3 us
  transfers between devices with their start and end apart: 7, of which 7 were waited for; matrix products, arithmetic and copies ran while one was open for 1% of the time, Pallas kernels for 0%

commit v1 on v0

v1 whole, which is shorter than its diff:
```python
import functools
import math

import jax
import jax.numpy as jnp
from jax import lax
from jax.experimental import pallas as pl
from jax.experimental.pallas import tpu as pltpu
from jax.sharding import PartitionSpec as P

STEPS = 2
MESH = pl.DeviceIdType.MESH

NY = 4
NZ = 8

PI_A = 3.1416015625
PI_B = -8.909031748771667e-06
PI_C = 1.2154188766544394e-10
SIN = (9.99999976e-01, -1.66666473e-01, 8.33289467e-03, -1.98005800e-04, 2.58984559e-06)


def scaled_cos(x, scale):
    q = jnp.round(x * (0.5 / math.pi))
    w = ((0.5 * x - q * PI_A) - q * PI_B) - q * PI_C
    w2 = w * w
    p = SIN[4]
    for c in SIN[3::-1]:
        p = p * w2 + c
    s = w * p
    return scale - (2.0 * scale) * (s * s)


def bytes_of(ref, sem):
    pltpu.make_async_copy(ref, ref, sem).wait()


def kernel(
    scale,
    e_ref, f_ref, ph_ref, w_ref, lab_ref,
    tr_ref, sc_ref,
    e_all, f_all, e_oth, e_two, f_rel,
    e_hi, e_lo, ft_hi, ft_lo, ph_t, ang, phi, lab_t,
    w_own, w_send, w_t,
    part, c_send, c_recv, l_send, l_recv, r_t,
    grad, g_send, g_recv, fin,
    e0_s, e0_r, ex_s, ex_r, er_s, er_r, ep_s, ep_r,
    fx_s, fx_r, fy_s, fy_r,
    w_s, w_r, c_s, c_r, l_s, l_r, r_s, r_r, rc_s, rc_r, g_s, g_r, q_s, q_r,
):
    clip = lax.axis_index("clip")
    feat = lax.axis_index("feat")
    c = lax.rem(feat, 2)
    xl = lax.rem(feat // 2, 2)
    z = feat // 4
    y = lax.rem(clip, NY)
    xh = clip // NY

    ke = e_ref.shape[0]
    kc = 4 * ke
    nf = f_ref.shape[1]
    nn = e_ref.shape[1]
    half = nn // 2
    quarter = nn // 4
    kk = w_ref.shape[0] * 8

    def feat_of(z_, xl_, c_):
        return (z_ * 2 + xl_) * 2 + c_

    def dev(clip_, feat_):
        return (clip_, feat_)

    partner = dev(clip, feat_of(z, xl, 1 - c))
    x_near = dev(clip, feat_of(z, 1 - xl, c))
    x_cross = dev((1 - xh) * NY + y, feat_of(z, 1 - xl, c))
    diag = dev(clip, feat_of(z, 1 - xl, 1 - c))

    def feat_peer(dz, dx):
        return lax.rem(z + dz, NZ), (1 - xl if dx else xl)

    feat_offsets = [(dz, dx) for dz in (4, 3, 5, 2, 6, 1, 7, 0) for dx in (1, 0) if (dz, dx) != (0, 0)]

    def clip_peer(d):
        return lax.rem(clip + d, 8)

    clip_offsets = [6, 2, 5, 7, 3, 1, 4]

    barrier = pltpu.get_barrier_semaphore()
    peers = [partner, x_cross, diag]
    for dz, dx in feat_offsets:
        pz, px = feat_peer(dz, dx)
        peers.append(dev(clip, feat_of(pz, px, c)))
    for d in clip_offsets:
        peers.append(dev(clip_peer(d), feat))
    for peer in peers:
        pl.semaphore_signal(barrier, inc=1, device_id=peer, device_id_type=MESH)

    w_own[...] = w_ref[...]
    w_send[0] = w_ref[...].astype(jnp.bfloat16)
    kw = w_ref.shape[0]
    my_rows = pl.ds(pl.multiple_of(clip * kw, kw), kw)
    w_t[0, my_rows, :] = w_ref[...].astype(jnp.bfloat16)

    pl.semaphore_wait(barrier, len(peers))

    sends = []

    def put(src, dst, s_sem, r_sem, to, own_sem=True):
        copy = pltpu.make_async_remote_copy(
            src_ref=src, dst_ref=dst, send_sem=s_sem, recv_sem=r_sem, device_id=to, device_id_type=MESH)
        copy.start()
        if own_sem:
            sends.append(copy)

    lanes_c = pl.ds(pl.multiple_of(c * half, half), half)
    lanes_o = pl.ds(pl.multiple_of((1 - c) * half, half), half)

    def e_rows(z_, xl_):
        return pl.ds(pl.multiple_of(z_ * kc + xl_ * (2 * ke), 8), 2 * ke)

    def e_piece(z_, xl_):
        return e_all.at[e_rows(z_, xl_), lanes_c]

    def f_rows(clip_, part_):
        if part_ is None:
            return f_all.at[pl.ds(pl.multiple_of(clip_ * kc, 8), kc), :]
        return f_all.at[pl.ds(pl.multiple_of(clip_ * kc + part_ * (kc // 2), 8), kc // 2), :]

    put(e_ref.at[:, lanes_o], e_oth, e0_s, e0_r, partner)

    hk = kc // 2
    put(f_ref.at[0:hk, :], f_rel.at[0], fx_s.at[0], fx_r.at[0], x_near)
    put(f_ref.at[hk:kc, :], f_rel.at[1], fx_s.at[1], fx_r.at[1], x_cross)
    y_right = dev(xh * NY + lax.rem(y + 1, NY), feat)
    y_left = dev(xh * NY + lax.rem(y + NY - 1, NY), feat)
    put(f_ref, f_rows(clip, None), fy_s.at[0, 0, 0], fy_r.at[0, 0, 0], y_right)
    put(f_ref, f_rows(clip, None), fy_s.at[1, 0, 0], fy_r.at[1, 0, 0], y_left)
    f_all[pl.ds(pl.multiple_of(clip * kc, 8), kc), :] = f_ref[...]

    for d in clip_offsets:
        put(w_send.at[0], w_t.at[0, my_rows, :], w_s.at[0], w_r.at[0], dev(clip_peer(d), feat), False)

    z_up = dev(clip, feat_of(lax.rem(z + 1, NZ), xl, c))
    z_down = dev(clip, feat_of(lax.rem(z + NZ - 1, NZ), xl, c))

    bytes_of(e_oth, e0_r)
    mine = e_ref[:, lanes_c]
    other = e_oth[...]
    first = c == 0
    e_two[0:ke, :] = jnp.where(first, mine, other)
    e_two[ke:2 * ke, :] = jnp.where(first, other, mine)
    e_all[e_rows(z, xl), lanes_c] = e_two[...]

    own_piece = e_piece(z, xl)
    put(own_piece, own_piece, ex_s, ex_r, x_near)
    put(own_piece, own_piece, er_s.at[0, 0, 0], er_r.at[0, 0, 0], z_up)
    put(own_piece, own_piece, er_s.at[1, 0, 0], er_r.at[1, 0, 0], z_down)

    def to_partner(z_, xl_, dz, o):
        put(e_piece(z_, xl_), e_piece(z_, xl_), ep_s.at[o, dz], ep_r.at[o, dz], partner)

    def split_e(z_, lanes):
        rows = pl.ds(pl.multiple_of(z_ * kc, 16), kc)
        x = e_all[rows, lanes]
        hi = x.astype(jnp.bfloat16)
        e_hi[rows, lanes] = hi
        e_lo[rows, lanes] = (x - hi.astype(jnp.float32)).astype(jnp.bfloat16)

    to_partner(z, xl, 0, 0)

    qn = pl.multiple_of((2 * c + xl) * quarter, quarter)
    lab_t[...] = lab_ref[pl.ds(qn, quarter), :].astype(jnp.float32).T
    ph_t[...] = jnp.broadcast_to(ph_ref[...], (128, nf)).T

    near_piece = e_piece(z, 1 - xl)
    bytes_of(near_piece, ex_r)
    put(near_piece, near_piece, er_s.at[0, 1, 0], er_r.at[0, 1, 0], z_up)
    put(near_piece, near_piece, er_s.at[1, 1, 0], er_r.at[1, 1, 0], z_down)
    to_partner(z, 1 - xl, 0, 1)
    split_e(z, lanes_c)

    def e_step(direction, o, s):
        dz = (NZ - s) if direction == 0 else s
        z_ = lax.rem(z + dz, NZ)
        xl_ = (1 - xl) if o else xl
        piece = e_piece(z_, xl_)
        bytes_of(piece, er_r.at[direction, o, s - 1])
        if s < 3 or (s == 3 and o == direction):
            put(piece, piece, er_s.at[direction, o, s], er_r.at[direction, o, s], z_up if direction == 0 else z_down)
        to_partner(z_, xl_, dz, o)

    xh_clip = (1 - xh) * NY + y

    def f_relay():
        bytes_of(f_rel.at[0], fx_r.at[0])
        put(f_rel.at[0], f_rows(xh_near_clip, 0), fx_s.at[2], fx_r.at[2], x_cross)
        bytes_of(f_rel.at[1], fx_r.at[1])
        put(f_rel.at[1], f_rows(xh_cross_clip, 1), fx_s.at[3], fx_r.at[3], x_near)

    xh_near_clip = clip
    xh_cross_clip = xh_clip

    def f_across():
        bytes_of(f_rows(xh_clip, 0), fx_r.at[2])
        bytes_of(f_rows(xh_clip, 1), fx_r.at[3])
        whole = f_rows(xh_clip, None)
        put(whole, whole, fy_s.at[0, 1, 0], fy_r.at[0, 1, 0], y_right)
        put(whole, whole, fy_s.at[1, 1, 0], fy_r.at[1, 1, 0], y_left)

    def f_turn(u):
        xh_ = (1 - xh) if u else xh
        from_left = xh_ * NY + lax.rem(y + NY - 1, NY)
        from_right = xh_ * NY + lax.rem(y + 1, NY)
        bytes_of(f_rows(from_left, None), fy_r.at[0, u, 0])
        put(f_rows(from_left, 0), f_rows(from_left, 0), fy_s.at[0, u, 1], fy_r.at[0, u, 1], y_right)
        bytes_of(f_rows(from_right, None), fy_r.at[1, u, 0])
        put(f_rows(from_right, 1), f_rows(from_right, 1), fy_s.at[1, u, 1], fy_r.at[1, u, 1], y_left)

    def f_last(u):
        xh_ = (1 - xh) if u else xh
        far = xh_ * NY + lax.rem(y + 2, NY)
        bytes_of(f_rows(far, 0), fy_r.at[0, u, 1])
        bytes_of(f_rows(far, 1), fy_r.at[1, u, 1])

    e_step(0, 0, 1)
    e_step(1, 0, 1)
    f_relay()
    e_step(0, 1, 1)
    e_step(1, 1, 1)
    split_e(lax.rem(z + NZ - 1, NZ), lanes_c)
    split_e(lax.rem(z + 1, NZ), lanes_c)
    f_turn(0)
    e_step(0, 0, 2)
    e_step(1, 0, 2)
    f_across()
    e_step(0, 1, 2)
    e_step(1, 1, 2)
    split_e(lax.rem(z + NZ - 2, NZ), lanes_c)
    split_e(lax.rem(z + 2, NZ), lanes_c)
    e_step(0, 0, 3)
    e_step(1, 0, 3)
    f_last(0)
    e_step(0, 1, 3)
    e_step(1, 1, 3)
    split_e(lax.rem(z + NZ - 3, NZ), lanes_c)
    split_e(lax.rem(z + 3, NZ), lanes_c)
    f_turn(1)
    e_step(0, 0, 4)
    e_step(1, 1, 4)
    split_e(lax.rem(z + 4, NZ), lanes_c)
    for dz in (0, 7, 1, 6, 2, 5, 3, 4):
        z_ = lax.rem(z + dz, NZ)
        for o in (0, 1):
            xl_ = (1 - xl) if o else xl
            bytes_of(e_all.at[e_rows(z_, xl_), lanes_o], ep_r.at[o, dz])
        split_e(z_, lanes_o)
    f_last(1)

    kt = e_all.shape[0]
    for b in range(kt // 128):
        x = f_all[128 * b:128 * b + 128, :].T
        hi = x.astype(jnp.bfloat16)
        ft_hi[:, 128 * b:128 * b + 128] = hi
        ft_lo[:, 128 * b:128 * b + 128] = (x - hi.astype(jnp.float32)).astype(jnp.bfloat16)

    dot = functools.partial(jnp.dot, preferred_element_type=jnp.float32)

    @pl.loop(0, nn // 256)
    def _(n):
        cols = pl.ds(pl.multiple_of(n * 256, 256), 256)
        ang[...] = dot(ft_hi[...], e_lo[:, cols]) + dot(ft_lo[...], e_hi[:, cols]) + dot(ft_hi[...], e_hi[:, cols])

        @pl.loop(0, nf // 32)
        def _(m):
            rows = pl.ds(pl.multiple_of(m * 32, 32), 32)
            p = ph_t[rows, :]
            x = ang[rows, :] + jnp.concatenate([p, p], axis=1)
            phi[rows, cols] = scaled_cos(x, scale).astype(jnp.bfloat16)

    my_block = pl.ds(pl.multiple_of(z * 16, 16), 16)
    my_lanes = pl.ds(pl.multiple_of(xl * quarter, quarter), quarter)

    def summed_logits(t):
        w = w_t[t]
        c_send[t] = dot(w, phi[:, lanes_o]).astype(jnp.bfloat16)
        put(c_send.at[t], c_recv.at[t], c_s.at[t], c_r.at[t], partner)
        part[...] = dot(w, phi[:, lanes_c])
        bytes_of(c_recv.at[t], c_r.at[t])
        total = part[...] + c_recv[t].astype(jnp.float32)
        part[...] = total
        l_send[t] = total.astype(jnp.bfloat16)
        for dz, dx in feat_offsets:
            pz, px = feat_peer(dz, dx)
            src = l_send.at[t, pl.ds(pl.multiple_of(pz * 16, 16), 16), pl.ds(pl.multiple_of(px * quarter, quarter), quarter)]
            put(src, l_recv.at[t, dx * NZ + dz - 1], l_s.at[t], l_r.at[t], dev(clip, feat_of(pz, px, c)), False)
        acc = part[my_block, my_lanes]
        bytes_of(l_recv.at[t], l_r.at[t])
        for i in range(2 * NZ - 1):
            acc = acc + l_recv[t, i].astype(jnp.float32)
        return acc

    nt = (((1,), (1,)), ((), ()))
    full_lanes = pl.ds(pl.multiple_of(c * half + xl * quarter, quarter), quarter)

    for t in range(STEPS):
        bytes_of(g_recv.at[0], w_r.at[t])
        acc = summed_logits(t)
        residual = (jax.nn.sigmoid(acc) - lab_t[my_block, :]).astype(jnp.bfloat16)
        r_t[t, my_block, full_lanes] = residual
        mine_r = r_t.at[t, my_block, full_lanes]
        for dz, dx in feat_offsets:
            pz, px = feat_peer(dz, dx)
            put(mine_r, mine_r, r_s.at[t], r_r.at[t], dev(clip, feat_of(pz, px, c)), False)
        bytes_of(l_recv.at[t], r_r.at[t])
        half_r = r_t.at[t, :, lanes_c]
        put(half_r, half_r, rc_s.at[t], rc_r.at[t], partner)
        grad[...] = lax.dot_general(r_t[t, :, lanes_c], phi[:, lanes_c], nt, preferred_element_type=jnp.float32)
        bytes_of(r_t.at[t, :, lanes_o], rc_r.at[t])
        total = grad[...] + lax.dot_general(r_t[t, :, lanes_o], phi[:, lanes_o], nt, preferred_element_type=jnp.float32)
        grad[...] = total
        g_send[t] = total.astype(jnp.bfloat16)
        for d in clip_offsets:
            j = clip_peer(d)
            put(g_send.at[t, pl.ds(pl.multiple_of(j * kw, kw), kw), :], g_recv.at[t, d - 1], g_s.at[t], g_r.at[t], dev(j, feat), False)
        g = grad[my_rows, :]
        bytes_of(g_recv.at[t], g_r.at[t])
        for i in range(7):
            g = g + g_recv[t, i].astype(jnp.float32)
        w_new = w_own[...] - 0.25 * g
        w_own[...] = w_new
        w_half = w_new.astype(jnp.bfloat16)
        w_send[t + 1] = w_half
        w_t[t + 1, my_rows, :] = w_half
        for d in clip_offsets:
            put(w_send.at[t + 1], w_t.at[t + 1, my_rows, :], w_s.at[t + 1], w_r.at[t + 1], dev(clip_peer(d), feat), False)
    tr_ref[...] = w_own[...]

    bytes_of(g_recv.at[0], w_r.at[STEPS])
    acc = summed_logits(STEPS)
    fin[:, full_lanes] = acc
    mine_f = fin.at[:, full_lanes]
    for to in (diag, x_near, partner):
        put(mine_f, mine_f, q_s, q_r, to, False)
    bytes_of(fin.at[:, 0:3 * quarter], q_r)
    which = 2 * xl + c
    out = fin[0:4, :]
    for i in range(1, 4):
        out = jnp.where(which == i, fin[4 * i:4 * i + 4, :], out)
    sc_ref[...] = out

    for copy in sends:
        copy.wait_send()
    for t in range(STEPS + 1):
        bytes_of(g_recv.at[0], w_s.at[t])
        bytes_of(l_recv.at[0], l_s.at[t])
    for t in range(STEPS):
        bytes_of(l_recv.at[0], r_s.at[t])
        bytes_of(g_recv.at[0], g_s.at[t])
    bytes_of(fin.at[:, 0:3 * quarter], q_s)


def per_device(embeds, frequencies, phases, weights, labels):
    nn, ke = embeds.shape
    kc, nf = frequencies.shape
    kw = weights.shape[1]
    kk = labels.shape[1]
    kt = kc * lax.axis_size("clip")
    total_features = nf * lax.axis_size("feat")
    scale = math.sqrt(2.0 / total_features)
    f32, b16 = jnp.float32, jnp.bfloat16
    dma = pltpu.SemaphoreType.DMA
    vm = pl.BlockSpec(memory_space=pltpu.VMEM)
    half, quarter = nn // 2, nn // 4
    steps = STEPS + 1
    scratch = [
        pltpu.VMEM((kt, nn), f32),
        pltpu.VMEM((kt, nf), f32),
        pltpu.VMEM((ke, half), f32),
        pltpu.VMEM((2 * ke, half), f32),
        pltpu.VMEM((2, kc // 2, nf), f32),
        pltpu.VMEM((kt, nn), b16),
        pltpu.VMEM((kt, nn), b16),
        pltpu.VMEM((nf, kt), b16),
        pltpu.VMEM((nf, kt), b16),
        pltpu.VMEM((nf, 128), f32),
        pltpu.VMEM((nf, 256), f32),
        pltpu.VMEM((nf, nn), b16),
        pltpu.VMEM((kk, quarter), f32),
        pltpu.VMEM((kw, nf), f32),
        pltpu.VMEM((steps, kw, nf), b16),
        pltpu.VMEM((steps, kk, nf), b16),
        pltpu.VMEM((kk, half), f32),
        pltpu.VMEM((steps, kk, half), b16),
        pltpu.VMEM((steps, kk, half), b16),
        pltpu.VMEM((steps, kk, half), b16),
        pltpu.VMEM((steps, 2 * NZ - 1, 16, quarter), b16),
        pltpu.VMEM((STEPS, kk, nn), b16),
        pltpu.VMEM((kk, nf), f32),
        pltpu.VMEM((STEPS, kk, nf), b16),
        pltpu.VMEM((STEPS, 7, kw, nf), b16),
        pltpu.VMEM((16, nn), f32),
        dma, dma, dma, dma, dma((2, 2, 4)), dma((2, 2, 4)), dma((2, NZ)), dma((2, NZ)),
        dma((4,)), dma((4,)), dma((2, 2, 2)), dma((2, 2, 2)),
        dma((steps,)), dma((steps,)), dma((steps,)), dma((steps,)), dma((steps,)), dma((steps,)),
        dma((STEPS,)), dma((STEPS,)), dma((STEPS,)), dma((STEPS,)), dma((STEPS,)), dma((STEPS,)), dma, dma,
    ]
    trained_t, scores_t = pl.pallas_call(
        functools.partial(kernel, scale),
        out_shape=(jax.ShapeDtypeStruct((kw, nf), f32), jax.ShapeDtypeStruct((4, nn), f32)),
        in_specs=[vm] * 5,
        out_specs=(vm, vm),
        scratch_shapes=scratch,
        compiler_params=pltpu.CompilerParams(
            collective_id=0, has_side_effects=True, vmem_limit_bytes=60 * 1024 * 1024),
    )(embeds.T, frequencies, phases[None, :], weights.T, labels)
    return trained_t.T, scores_t.T


def solution(mesh):
    placed = (P("clip", "feat"), P("clip", "feat"), P("feat"), P("feat", "clip"), P("clip", None))
    return jax.shard_map(
        per_device,
        mesh=mesh,
        in_specs=placed,
        out_specs=(P("feat", "clip"), P("clip", "feat")),
        check_vma=False,
    )
```

time: 1090 us -> 119 us (0.11)
  waiting for transfers between devices: 954 us -> 0 us
  Pallas kernels: 0 us -> 115 us
  blocking collectives: 85.1 us -> 0 us
  matrix products: 31.7 us -> 0 us
  between operations: 14.2 us -> 0.65 us
    psum x3 -> x0, waiting for transfers between devices: 696 us -> none  [summed_logits(): return lax.psum(partial_value, 'feat')]
    reduce_scatter x2 -> x0, waiting for transfers between devices: 152 us -> none  [per_device(): lax.psum_scatter(grad_part, 'clip', scatter_dimension=1, tiled=True)]
    pallas_call x0 -> x1, Pallas kernels: none -> 115 us  [per_device(): pl.pallas_call(functools.partial(kernel, scale), out_shape=(jax.ShapeDtyp...]
    all_gather x2 -> x0, waiting for transfers between devices: 105 us -> none  [the longest x1 61.4 us: per_device(): freq_full = lax.all_gather(frequencies, 'clip', axis=0, tiled=True)]
    all_gather x3 -> x0, blocking collectives: 85.1 us -> none  [the longest x2 55.7 us: per_device(): lax.all_gather(own_weights.astype(jnp.bfloat16), 'clip', axis=1, tiled=True)]
    dot_general x6 -> x0, matrix products: 31.7 us -> none  [the longest x1 23.3 us: per_device(): jnp.dot(lax.all_gather(embeds, 'feat', axis=1, tiled=True), freq_full, pr...]
  transfers between devices with their start and end apart: 7 -> 0, of which waited for: 7 -> 0; matrix products, arithmetic and copies ran while one was open for 1% -> 0% of each run, Pallas kernels for 0% -> 0%
where the time goes in v1:
time: 119 us
  Pallas kernels  115 us (97%)
  local copies, waits for them, and re-layouts  3.28 us (3%)
    pallas_call x1, Pallas kernels, per_device(): pl.pallas_call(functools.partial(kernel, scale), out_shape=(jax.ShapeDtyp...  115 us

profile of v1, /device:TPU:1, one launch (start us, length us, event | category | flops | bytes accessed | tf_op | source)
XLA Modules:
  0.0 119.2 jit_solution(10783282855596499496)
XLA Ops:
  0.6 1.3 %broadcast_in_dim.3.ph_ref = f32[1,640]{1,0:T(1,128)} reshape(f32[640]{0:T(1024)} %param.7) | data formatting | bytes 5120 | tf_op jit(solution)/shard_map/broadcast_in_dim | solution.py:415
  1.9 115.2 %shard_map.68 = (f32[16,640]{1,0:T(8,128)}, f32[4,1024]{1,0:T(4,128)}) custom-call(f32[36,1024]{1,0:T(8,128)} %bitcast.4, f32[144,640]{1,0:T(8,128)} %f_ref.1, f32[1,640]{1,0:T(1,128)} %broadcast_in_dim.3.ph_ref, f32[16,640]{1,0:T(8,128)} %bitcast.5, s32[1024,128]{1,0:T(8,128)} %lab_ref.1), custom_call_target="tpu_custom_call" | custom-call | tf_op jit(solution)/shard_map/pallas_call | solution.py:407
  117.1 0.0 copy-start
  117.1 1.4 %copy.9 = f32[640,16]{0,1:T(8,128)} copy(f32[640,16]{0,1:T(8,128)} %bitcast.6) | data formatting | bytes 81920
  118.6 0.0 copy-done
  118.6 0.6 copy.10
Async XLA Ops:
  117.1 1.4 %copy-start = (f32[4,1024]{1,0:T(4,128)S(1)}, f32[4,1024]{1,0:T(4,128)}, u32[]{:S(2)}) copy-start(f32[4,1024]{1,0:T(4,128)} %get-tuple-element.5) | copy-start | bytes 49156

commit v2 on v1

v2 whole, which is shorter than its diff:
```python
import functools
import math

import jax
import jax.numpy as jnp
from jax import lax
from jax.experimental import pallas as pl
from jax.experimental.pallas import tpu as pltpu
from jax.sharding import PartitionSpec as P

STEPS = 2
MESH = pl.DeviceIdType.MESH

NY = 4
NZ = 8

PI_A = 3.1416015625
PI_B = -8.909031748771667e-06
PI_C = 1.2154188766544394e-10
SIN = (9.99999976e-01, -1.66666473e-01, 8.33289467e-03, -1.98005800e-04, 2.58984559e-06)


def scaled_cos(x, scale):
    q = jnp.round(x * (0.5 / math.pi))
    w = ((0.5 * x - q * PI_A) - q * PI_B) - q * PI_C
    w2 = w * w
    p = SIN[4]
    for c in SIN[3::-1]:
        p = p * w2 + c
    s = w * p
    return scale - (2.0 * scale) * (s * s)


def bytes_of(ref, sem):
    pltpu.make_async_copy(ref, ref, sem).wait()


def kernel(
    scale,
    e_ref, f_ref, ph_ref, w_ref, lab_ref,
    tr_ref, sc_ref,
    e_all, f_all, e_raw, e_two, f_rel,
    e3, f3, ang, phi, lab_t,
    w_own, w_send, w_t,
    part, c_send, c_recv, l_send, l_recv, r_t,
    grad, g_send, g_recv,
    eq_s, eq_r, er_s, er_r, ep_s, ep_r,
    fx_s, fx_r, fy_s, fy_r,
    w_s, w_r, c_s, c_r, l_s, l_r, r_s, r_r, rc_s, rc_r, g_s, g_r,
):
    clip = lax.axis_index("clip")
    feat = lax.axis_index("feat")
    c = lax.rem(feat, 2)
    xl = lax.rem(feat // 2, 2)
    z = feat // 4
    y = lax.rem(clip, NY)
    xh = clip // NY

    ke = e_ref.shape[0]
    kc = 4 * ke
    nf = f_ref.shape[1]
    nn = e_ref.shape[1]
    half = nn // 2
    quarter = nn // 4
    kw = w_ref.shape[0]

    def feat_of(z_, xl_, c_):
        return (z_ * 2 + xl_) * 2 + c_

    def clip_of(u, dy):
        return ((1 - xh) if u else xh) * NY + lax.rem(y + dy, NY)

    partner = (clip, feat_of(z, xl, 1 - c))
    x_near = (clip, feat_of(z, 1 - xl, c))
    diag = (clip, feat_of(z, 1 - xl, 1 - c))
    x_cross = (clip_of(1, 0), feat_of(z, 1 - xl, c))
    y_right = (clip_of(0, 1), feat)
    y_left = (clip_of(0, NY - 1), feat)
    z_up = (clip, feat_of(lax.rem(z + 1, NZ), xl, c))
    z_down = (clip, feat_of(lax.rem(z + NZ - 1, NZ), xl, c))

    def feat_peer(dz, dx):
        return lax.rem(z + dz, NZ), (1 - xl if dx else xl)

    feat_offsets = [(dz, dx) for dz in (4, 3, 5, 2, 6, 1, 7, 0) for dx in (1, 0) if (dz, dx) != (0, 0)]
    clip_offsets = [(u, dy) for dy in (2, 1, 3, 0) for u in (1, 0) if (u, dy) != (0, 0)]

    def slot_of(u, dy):
        return u * NY + dy - 1

    barrier = pltpu.get_barrier_semaphore()
    neighbours = [partner, x_near, x_cross, diag, z_up, z_down, y_right, y_left]
    for peer in neighbours:
        pl.semaphore_signal(barrier, inc=1, device_id=peer, device_id_type=MESH)

    my_rows = pl.ds(pl.multiple_of(clip * kw, kw), kw)
    w_own[...] = w_ref[...]
    w_send[0] = w_ref[...].astype(jnp.bfloat16)
    w_t[0, my_rows, :] = w_ref[...].astype(jnp.bfloat16)

    pl.semaphore_wait(barrier, len(neighbours))

    sends = []

    def put(src, dst, s_sem, r_sem, to, own_sem=True):
        copy = pltpu.make_async_remote_copy(
            src_ref=src, dst_ref=dst, send_sem=s_sem, recv_sem=r_sem, device_id=to, device_id_type=MESH)
        copy.start()
        if own_sem:
            sends.append(copy)

    lanes_c = pl.ds(pl.multiple_of(c * half, half), half)
    lanes_o = pl.ds(pl.multiple_of((1 - c) * half, half), half)

    def e_rows(z_, xl_):
        return pl.ds(pl.multiple_of(z_ * kc + xl_ * (2 * ke), 8), 2 * ke)

    def e_piece(z_, xl_):
        return e_all.at[e_rows(z_, xl_), lanes_c]

    def f_block(clip_, lo, hi):
        return f_all.at[pl.ds(pl.multiple_of(clip_ * kc + lo, 8), hi - lo), :]

    def send_w(u, dy):
        put(w_send.at[0], w_t.at[0, my_rows, :], w_s.at[0], w_r.at[0], (clip_of(u, dy), feat), False)

    put(e_ref.at[:, lanes_o], e_raw.at[0], eq_s.at[0], eq_r.at[0], partner)
    put(e_ref.at[:, lanes_c], e_raw.at[1], eq_s.at[1], eq_r.at[1], x_near)
    put(e_ref.at[:, lanes_o], e_raw.at[2], eq_s.at[2], eq_r.at[2], diag)

    cut = kc // 3
    mid = kc // 2
    put(f_ref.at[cut:kc, :], f_rel.at[cut:kc, :], fx_s.at[1], fx_r.at[1], x_cross)
    put(f_ref.at[0:cut, :], f_rel.at[0:cut, :], fx_s.at[0], fx_r.at[0], x_near)
    lows = (0, mid)

    def f_send(direction, u, k, clip_, lo, hi, src=None):
        dst = f_block(clip_, lo, hi)
        put(dst if src is None else src, dst, fy_s.at[direction, u, k], fy_r.at[direction, u, k],
            y_right if direction == 0 else y_left)

    for k in (0, 1):
        for direction in (0, 1):
            lo = lows[k ^ direction]
            f_send(direction, 0, k, clip, lo, lo + mid, f_ref.at[lo:lo + mid, :])
    for dy in (1, 3):
        send_w(0, dy)

    def join(own, oth):
        first = c == 0
        e_two[0:ke, :] = jnp.where(first, own, oth)
        e_two[ke:2 * ke, :] = jnp.where(first, oth, own)
        return e_two[...]

    def e_start(o, xl_):
        piece = e_piece(z, xl_)
        put(piece, piece, er_s.at[0, o, 0], er_r.at[0, o, 0], z_up)
        put(piece, piece, er_s.at[1, o, 0], er_r.at[1, o, 0], z_down)
        put(piece, piece, ep_s.at[o, 0], ep_r.at[0], partner)

    bytes_of(e_raw.at[0], eq_r.at[0])
    e_all[e_rows(z, xl), lanes_c] = join(e_ref[:, lanes_c], e_raw[0])
    e_start(0, xl)

    f_all[pl.ds(pl.multiple_of(clip * kc, 8), kc), :] = f_ref[...]
    qn = pl.multiple_of((2 * c + xl) * quarter, quarter)
    lab_t[...] = lab_ref[pl.ds(qn, quarter), :].astype(jnp.float32).T
    for b in range(nf // 128):
        column = jnp.broadcast_to(ph_ref[b:b + 1, :], (128, 128)).T
        for n in range(nn // 128):
            ang[128 * b:128 * b + 128, 128 * n:128 * n + 128] = column

    bytes_of(e_raw.at[1], eq_r.at[1])
    bytes_of(e_raw.at[2], eq_r.at[2])
    e_all[e_rows(z, 1 - xl), lanes_c] = join(e_raw[1], e_raw[2])
    e_start(1, 1 - xl)

    def e_step(direction, o, s):
        dz = (NZ - s) if direction == 0 else s
        z_ = lax.rem(z + dz, NZ)
        xl_ = (1 - xl) if o else xl
        piece = e_piece(z_, xl_)
        bytes_of(piece, er_r.at[direction, o, s - 1])
        if s < 3 or (s == 3 and o == direction):
            put(piece, piece, er_s.at[direction, o, s], er_r.at[direction, o, s], z_up if direction == 0 else z_down)
        put(piece, piece, ep_s.at[o, dz], ep_r.at[dz], partner)

    def e_prep(dz, lanes):
        z_ = lax.rem(z + dz, NZ)
        x = e_all[pl.ds(pl.multiple_of(z_ * kc, 16), kc), lanes]
        hi = x.astype(jnp.bfloat16)
        e3[z_, 0:kc, lanes] = hi
        e3[z_, kc:2 * kc, lanes] = (x - hi.astype(jnp.float32)).astype(jnp.bfloat16)
        e3[z_, 2 * kc:3 * kc, lanes] = hi

    def e_other(dz):
        z_ = lax.rem(z + dz, NZ)
        bytes_of(e_all.at[pl.ds(pl.multiple_of(z_ * kc, 16), kc), lanes_o], ep_r.at[dz])
        e_prep(dz, lanes_o)

    def f_prep(u, dy):
        j = clip_of(u, dy)
        x = f_all[pl.ds(pl.multiple_of(j * kc, 16), kc), :]
        hi = x.astype(jnp.bfloat16)
        lo = (x - hi.astype(jnp.float32)).astype(jnp.bfloat16)
        f3[j] = jnp.concatenate([hi, hi, lo], axis=0).T

    def f_wait(direction, u, k, clip_, lo, hi):
        bytes_of(f_block(clip_, lo, hi), fy_r.at[direction, u, k])

    dot = functools.partial(jnp.dot, preferred_element_type=jnp.float32)

    def stage_of(j):
        up = lax.rem(j - z + NZ, NZ)
        e_turn = jnp.minimum(up, NZ - up)
        right = lax.rem(lax.rem(j, NY) - y + NY, NY)
        away = jnp.minimum(right, NY - right)
        f_turn = jnp.where(j // NY == xh, away, 2 + away + away // 2)
        return jnp.maximum(e_turn, f_turn)

    def products(stage, first, last):
        @pl.loop(first, last)
        def _(j):
            @pl.when(stage_of(j) == stage)
            def _():
                @pl.loop(0, nn // 256)
                def _(n):
                    cols = pl.ds(pl.multiple_of(n * 256, 256), 256)
                    ang[:, cols] = ang[:, cols] + dot(f3[j], e3[j, :, cols])

    e_step(0, 0, 1)
    e_step(1, 0, 1)
    f_wait(0, 0, 0, clip_of(0, 3), 0, mid)
    f_send(0, 0, 2, clip_of(0, 3), 0, mid)
    f_wait(1, 0, 0, clip_of(0, 1), mid, kc)
    f_send(1, 0, 2, clip_of(0, 1), mid, kc)
    bytes_of(f_rel.at[cut:kc, :], fx_r.at[1])
    put(f_rel.at[cut:kc, :], f_block(clip_of(1, 0), cut, kc), fx_s.at[3], fx_r.at[3], x_near)
    bytes_of(f_rel.at[0:cut, :], fx_r.at[0])
    put(f_rel.at[0:cut, :], f_block(clip, 0, cut), fx_s.at[2], fx_r.at[2], x_cross)
    e_prep(0, lanes_c)
    f_prep(0, 0)
    e_other(0)
    products(0, 0, 8)
    e_step(0, 1, 1)
    e_step(1, 1, 1)
    e_prep(1, lanes_c)
    e_prep(7, lanes_c)
    e_step(0, 0, 2)
    e_step(1, 0, 2)
    f_wait(0, 0, 1, clip_of(0, 3), mid, kc)
    f_wait(1, 0, 1, clip_of(0, 1), 0, mid)
    over = clip_of(1, 0)
    bytes_of(f_block(over, 0, cut), fx_r.at[2])
    f_send(0, 1, 0, over, 0, cut)
    f_send(1, 1, 0, over, 0, cut)
    bytes_of(f_block(over, cut, kc), fx_r.at[3])
    f_send(0, 1, 1, over, cut, mid)
    f_send(1, 1, 1, over, mid, kc)
    f_send(0, 1, 2, over, mid, kc)
    f_send(1, 1, 2, over, cut, mid)
    send_w(1, 0)
    f_prep(0, 1)
    f_prep(0, 3)
    e_step(0, 1, 2)
    e_step(1, 1, 2)
    e_other(1)
    e_other(7)
    products(1, 0, 8)
    e_prep(2, lanes_c)
    e_prep(6, lanes_c)
    f_wait(0, 0, 2, clip_of(0, 2), 0, mid)
    f_wait(1, 0, 2, clip_of(0, 2), mid, kc)
    send_w(0, 2)
    f_prep(0, 2)
    f_prep(1, 0)
    e_step(0, 0, 3)
    e_step(1, 0, 3)
    e_other(2)
    e_other(6)
    f_wait(0, 1, 0, clip_of(1, 3), 0, cut)
    f_wait(0, 1, 1, clip_of(1, 3), cut, mid)
    f_send(0, 1, 3, clip_of(1, 3), 0, mid)
    f_wait(1, 1, 0, clip_of(1, 1), 0, cut)
    f_wait(1, 1, 1, clip_of(1, 1), mid, kc)
    f_send(1, 1, 3, clip_of(1, 1), mid, kc)
    products(2, 0, 4)
    e_step(0, 1, 3)
    e_step(1, 1, 3)
    products(2, 4, 8)
    e_prep(3, lanes_c)
    e_prep(5, lanes_c)
    f_wait(0, 1, 2, clip_of(1, 3), mid, kc)
    f_wait(1, 1, 2, clip_of(1, 1), cut, mid)
    send_w(1, 1)
    send_w(1, 3)
    f_prep(1, 1)
    f_prep(1, 3)
    e_step(0, 0, 4)
    e_step(1, 1, 4)
    e_prep(4, lanes_c)
    e_other(3)
    e_other(5)
    products(3, 0, 8)
    e_other(4)
    products(4, 0, 8)
    last_block = clip_of(1, 2)
    f_wait(0, 1, 3, last_block, 0, mid)
    f_wait(1, 1, 3, last_block, mid, kc)
    send_w(1, 2)
    f_prep(1, 2)

    @pl.loop(0, nn // 256)
    def _(n):
        cols = pl.ds(pl.multiple_of(n * 256, 256), 256)
        for m in range(nf // 128):
            rows = slice(128 * m, 128 * m + 128)
            x = ang[rows, cols] + dot(f3[last_block, rows, :], e3[last_block, :, cols])
            phi[rows, cols] = scaled_cos(x, scale).astype(jnp.bfloat16)

    my_block = pl.ds(pl.multiple_of(z * 16, 16), 16)
    my_lanes = pl.ds(pl.multiple_of(xl * quarter, quarter), quarter)

    def exchange(t, source, own):
        for dz, dx in feat_offsets:
            pz, px = feat_peer(dz, dx)
            put(source(pz, px), l_recv.at[t, dx * NZ + dz - 1], l_s.at[t], l_r.at[t], (clip, feat_of(pz, px, c)), False)
        acc = own()
        bytes_of(l_recv.at[t], l_r.at[t])
        for i in range(2 * NZ - 1):
            acc = acc + l_recv[t, i].astype(jnp.float32)
        return acc

    def summed_logits(t):
        w = w_t[t]
        c_send[t] = dot(w, phi[:, lanes_o]).astype(jnp.bfloat16)
        put(c_send.at[t], c_recv.at[t], c_s.at[t], c_r.at[t], partner)
        part[...] = dot(w, phi[:, lanes_c])
        bytes_of(c_recv.at[t], c_r.at[t])
        total = part[...] + c_recv[t].astype(jnp.float32)
        part[...] = total
        l_send[t] = total.astype(jnp.bfloat16)

        def source(pz, px):
            return l_send.at[t, pl.ds(pl.multiple_of(pz * 16, 16), 16), pl.ds(pl.multiple_of(px * quarter, quarter), quarter)]

        return exchange(t, source, lambda: part[my_block, my_lanes])

    nt = (((1,), (1,)), ((), ()))
    full_lanes = pl.ds(pl.multiple_of(c * half + xl * quarter, quarter), quarter)

    for t in range(STEPS):
        bytes_of(g_recv.at[0], w_r.at[t])
        acc = summed_logits(t)
        residual = (jax.nn.sigmoid(acc) - lab_t[my_block, :]).astype(jnp.bfloat16)
        r_t[t, my_block, full_lanes] = residual
        mine_r = r_t.at[t, my_block, full_lanes]
        for dz, dx in feat_offsets:
            pz, px = feat_peer(dz, dx)
            put(mine_r, mine_r, r_s.at[t], r_r.at[t], (clip, feat_of(pz, px, c)), False)
        bytes_of(l_recv.at[t], r_r.at[t])
        half_r = r_t.at[t, :, lanes_c]
        put(half_r, half_r, rc_s.at[t], rc_r.at[t], partner)
        grad[...] = lax.dot_general(r_t[t, :, lanes_c], phi[:, lanes_c], nt, preferred_element_type=jnp.float32)
        bytes_of(r_t.at[t, :, lanes_o], rc_r.at[t])
        total = grad[...] + lax.dot_general(r_t[t, :, lanes_o], phi[:, lanes_o], nt, preferred_element_type=jnp.float32)
        grad[...] = total
        g_send[t] = total.astype(jnp.bfloat16)
        for u, dy in clip_offsets:
            j = clip_of(u, dy)
            put(g_send.at[t, pl.ds(pl.multiple_of(j * kw, kw), kw), :], g_recv.at[t, slot_of(u, dy)], g_s.at[t], g_r.at[t], (j, feat), False)
        g = grad[my_rows, :]
        bytes_of(g_recv.at[t], g_r.at[t])
        for i in range(7):
            g = g + g_recv[t, i].astype(jnp.float32)
        w_new = w_own[...] - 0.25 * g
        w_own[...] = w_new
        w_half = w_new.astype(jnp.bfloat16)
        w_send[t + 1] = w_half
        w_t[t + 1, my_rows, :] = w_half
        for u, dy in clip_offsets:
            put(w_send.at[t + 1], w_t.at[t + 1, my_rows, :], w_s.at[t + 1], w_r.at[t + 1], (clip_of(u, dy), feat), False)
    tr_ref[...] = w_own[...]

    t = STEPS
    bytes_of(g_recv.at[0], w_r.at[t])
    row = lax.broadcasted_iota(jnp.int32, (2 * 128, 128), 0)
    col = lax.broadcasted_iota(jnp.int32, (2 * 128, 128), 1)
    row_q = lax.broadcasted_iota(jnp.int32, (2 * 128, 1), 0) // 4 % 4

    def chip_blocks(core):
        pick = col == 8 * (row // 16) + 4 * core + row % 4
        w = dot(pick.astype(jnp.float32).astype(jnp.bfloat16), w_t[t])
        out = jnp.zeros((2 * 128, quarter), jnp.float32)
        for q in range(4):
            w_q = jnp.where(row_q == q, w, 0.0).astype(jnp.bfloat16)
            out = out + dot(w_q, phi[:, q * quarter:(q + 1) * quarter])
        return out

    out = chip_blocks(1 - c).astype(jnp.bfloat16)
    l_send[t, :, 0:quarter] = out[0:128, :]
    l_send[t, :, quarter:half] = out[128:256, :]
    put(l_send.at[t], c_recv.at[t], c_s.at[t], c_r.at[t], partner)
    out = chip_blocks(c)
    bytes_of(c_recv.at[t], c_r.at[t])
    for h in range(2):
        lanes = slice(h * quarter, (h + 1) * quarter)
        total = out[128 * h:128 * h + 128, :] + c_recv[t, :, lanes].astype(jnp.float32)
        part[:, lanes] = total
        c_send[t, :, lanes] = total.astype(jnp.bfloat16)

    def block_of(z_, xl_):
        i = 2 * z_ + xl_
        return pl.ds(pl.multiple_of(lax.rem(i, 8) * 16, 16), 16), pl.ds(pl.multiple_of(i // 8 * quarter, quarter), quarter)

    acc = exchange(t, lambda pz, px: c_send.at[(t, *block_of(pz, px))], lambda: part[block_of(z, xl)])
    for q in range(4):
        sc_ref[:, q * quarter:(q + 1) * quarter] = acc[4 * q:4 * q + 4, :]

    for copy in sends:
        copy.wait_send()
    for t in range(STEPS + 1):
        bytes_of(g_recv.at[0], w_s.at[t])
        bytes_of(l_recv.at[0], l_s.at[t])
    for t in range(STEPS):
        bytes_of(l_recv.at[0], r_s.at[t])
        bytes_of(g_recv.at[0], g_s.at[t])


def per_device(embeds, frequencies, phases, weights, labels):
    nn, ke = embeds.shape
    kc, nf = frequencies.shape
    kw = weights.shape[1]
    kk = labels.shape[1]
    kt = kc * lax.axis_size("clip")
    total_features = nf * lax.axis_size("feat")
    scale = math.sqrt(2.0 / total_features)
    f32, b16 = jnp.float32, jnp.bfloat16
    dma = pltpu.SemaphoreType.DMA
    vm = pl.BlockSpec(memory_space=pltpu.VMEM)
    half, quarter = nn // 2, nn // 4
    steps = STEPS + 1
    scratch = [
        pltpu.VMEM((kt, nn), f32),
        pltpu.VMEM((kt, nf), f32),
        pltpu.VMEM((3, ke, half), f32),
        pltpu.VMEM((2 * ke, half), f32),
        pltpu.VMEM((kc, nf), f32),
        pltpu.VMEM((8, 3 * kc, nn), b16),
        pltpu.VMEM((8, nf, 3 * kc), b16),
        pltpu.VMEM((nf, nn), f32),
        pltpu.VMEM((nf, nn), b16),
        pltpu.VMEM((kk, quarter), f32),
        pltpu.VMEM((kw, nf), f32),
        pltpu.VMEM((steps, kw, nf), b16),
        pltpu.VMEM((steps, kk, nf), b16),
        pltpu.VMEM((kk, half), f32),
        pltpu.VMEM((steps, kk, half), b16),
        pltpu.VMEM((steps, kk, half), b16),
        pltpu.VMEM((steps, kk, half), b16),
        pltpu.VMEM((steps, 2 * NZ - 1, 16, quarter), b16),
        pltpu.VMEM((STEPS, kk, nn), b16),
        pltpu.VMEM((kk, nf), f32),
        pltpu.VMEM((STEPS, kk, nf), b16),
        pltpu.VMEM((STEPS, 7, kw, nf), b16),
        dma((3,)), dma((3,)), dma((2, 2, 4)), dma((2, 2, 4)), dma((2, NZ)), dma((NZ,)),
        dma((4,)), dma((4,)), dma((2, 2, 4)), dma((2, 2, 4)),
        dma((steps,)), dma((steps,)), dma((steps,)), dma((steps,)), dma((steps,)), dma((steps,)),
        dma((STEPS,)), dma((STEPS,)), dma((STEPS,)), dma((STEPS,)), dma((STEPS,)), dma((STEPS,)),
    ]
    trained_t, scores_t = pl.pallas_call(
        functools.partial(kernel, scale),
        out_shape=(jax.ShapeDtypeStruct((kw, nf), f32), jax.ShapeDtypeStruct((4, nn), f32)),
        in_specs=[vm] * 5,
        out_specs=(vm, vm),
        scratch_shapes=scratch,
        compiler_params=pltpu.CompilerParams(
            collective_id=0, has_side_effects=True, vmem_limit_bytes=60 * 1024 * 1024),
    )(embeds.T, frequencies, phases.reshape(nf // 128, 128), weights.T, labels)
    return trained_t.T, scores_t.T


def solution(mesh):
    placed = (P("clip", "feat"), P("clip", "feat"), P("feat"), P("feat", "clip"), P("clip", None))
    return jax.shard_map(
        per_device,
        mesh=mesh,
        in_specs=placed,
        out_specs=(P("feat", "clip"), P("clip", "feat")),
        check_vma=False,
    )
```

time: 119 us -> 112 us (0.941)
  Pallas kernels: 115 us -> 109 us
  local copies, waits for them, and re-layouts: 3.28 us -> 2.01 us
    pallas_call x1, Pallas kernels: 115 us -> 109 us  [per_device(): pl.pallas_call(functools.partial(kernel, scale), out_shape=(jax.ShapeDtyp...]
    broadcast_in_dim x1 -> x0, local copies, waits for them, and re-layouts: 1.27 us -> none  [per_device(): phases[None, :]]
where the time goes in v2:
time: 112 us
  Pallas kernels  109 us (97%)
  local copies, waits for them, and re-layouts  2.01 us (2%)
    pallas_call x1, Pallas kernels, per_device(): pl.pallas_call(functools.partial(kernel, scale), out_shape=(jax.ShapeDtyp...  109 us

profile of v2, /device:TPU:1, one launch (start us, length us, event | category | flops | bytes accessed | tf_op | source)
XLA Modules:
  0.0 112.2 jit_solution(10002280756747615524)
XLA Ops:
  0.6 109.5 %shard_map.68 = (f32[16,640]{1,0:T(8,128)}, f32[4,1024]{1,0:T(4,128)}) custom-call(f32[36,1024]{1,0:T(8,128)} %bitcast.5, f32[144,640]{1,0:T(8,128)} %f_ref.1, f32[5,128]{1,0:T(8,128)} %bitcast.9, f32[16,640]{1,0:T(8,128)} %bitcast.6, s32[1024,128]{1,0:T(8,128)} %lab_ref.1), custom_call_target="tpu_custom_call" | custom-call | tf_op jit(solution)/shard_map/pallas_call | solution.py:471
  110.1 0.0 copy-start
  110.1 1.4 %copy.9 = f32[640,16]{0,1:T(8,128)} copy(f32[640,16]{0,1:T(8,128)} %bitcast.7) | data formatting | bytes 81920
  111.5 0.0 copy-done
  111.5 0.6 copy.10
Async XLA Ops:
  110.1 1.4 %copy-start = (f32[4,1024]{1,0:T(4,128)S(1)}, f32[4,1024]{1,0:T(4,128)}, u32[]{:S(2)}) copy-start(f32[4,1024]{1,0:T(4,128)} %get-tuple-element.5) | copy-start | bytes 49156

commit v3 on v2

--- a/solution.py
+++ b/solution.py
@@ -37,17 +37,27 @@
 
 def kernel(
     scale,
-    e_ref, f_ref, ph_ref, w_ref, lab_ref,
-    tr_ref, sc_ref,
+    e_hbm, f_hbm, ph_hbm, w_hbm, lab_hbm,
+    tr_hbm, sc_hbm,
+    e_ref, f_ref, ph_ref, w_ref, lab_ref, sc_ref, picks,
     e_all, f_all, e_raw, e_two, f_rel,
     e3, f3, ang, phi, lab_t,
     w_own, w_send, w_t,
     part, c_send, c_recv, l_send, l_recv, r_t,
-    grad, g_send, g_recv,
+    grad, g_send, g_recv, logits,
     eq_s, eq_r, er_s, er_r, ep_s, ep_r,
     fx_s, fx_r, fy_s, fy_r,
     w_s, w_r, c_s, c_r, l_s, l_r, r_s, r_r, rc_s, rc_r, g_s, g_r,
+    in_s, out_s, hello,
 ):
+    loads = [
+        pltpu.make_async_copy(src, dst, in_s.at[i])
+        for i, (src, dst) in enumerate(
+            ((e_hbm, e_ref), (f_hbm, f_ref), (w_hbm, w_ref), (ph_hbm, ph_ref), (lab_hbm, lab_ref)))
+    ]
+    for load in loads:
+        load.start()
+
     clip = lax.axis_index("clip")
     feat = lax.axis_index("feat")
     c = lax.rem(feat, 2)
@@ -94,12 +104,22 @@
         pl.semaphore_signal(barrier, inc=1, device_id=peer, device_id_type=MESH)
 
     my_rows = pl.ds(pl.multiple_of(clip * kw, kw), kw)
+    for load in loads[0:3]:
+        load.wait()
     w_own[...] = w_ref[...]
     w_send[0] = w_ref[...].astype(jnp.bfloat16)
     w_t[0, my_rows, :] = w_ref[...].astype(jnp.bfloat16)
 
     pl.semaphore_wait(barrier, len(neighbours))
 
+    def greet(n):
+        for peer in (x_near, x_cross, y_right, y_left):
+            pl.semaphore_signal(hello.at[n], inc=1, device_id=peer, device_id_type=MESH)
+
+    def greeted(n):
+        pl.semaphore_wait(hello.at[n], 4)
+
+    greet(0)
     sends = []
 
     def put(src, dst, s_sem, r_sem, to, own_sem=True):
@@ -143,8 +163,8 @@
         for direction in (0, 1):
             lo = lows[k ^ direction]
             f_send(direction, 0, k, clip, lo, lo + mid, f_ref.at[lo:lo + mid, :])
-    for dy in (1, 3):
-        send_w(0, dy)
+    greeted(0)
+    greet(1)
 
     def join(own, oth):
         first = c == 0
@@ -162,13 +182,27 @@
     e_all[e_rows(z, xl), lanes_c] = join(e_ref[:, lanes_c], e_raw[0])
     e_start(0, xl)
 
+    greeted(1)
+    greet(2)
+    for load in loads[3:]:
+        load.wait()
     f_all[pl.ds(pl.multiple_of(clip * kc, 8), kc), :] = f_ref[...]
+    row = lax.broadcasted_iota(jnp.int32, (2 * 128, 128), 0)
+    col = lax.broadcasted_iota(jnp.int32, (2 * 128, 128), 1)
+    for core in range(2):
+        there = col == 8 * (row // 16) + 4 * core + row % 4
+        for q in range(4):
+            pick = there & (row // 4 % 4 == q)
+            picks[core, q] = jnp.where(pick, 1.0, 0.0).astype(jnp.bfloat16)
     qn = pl.multiple_of((2 * c + xl) * quarter, quarter)
     lab_t[...] = lab_ref[pl.ds(qn, quarter), :].astype(jnp.float32).T
     for b in range(nf // 128):
         column = jnp.broadcast_to(ph_ref[b:b + 1, :], (128, 128)).T
         for n in range(nn // 128):
             ang[128 * b:128 * b + 128, 128 * n:128 * n + 128] = column
+    greeted(2)
+    for u, dy in clip_offsets:
+        send_w(u, dy)
 
     bytes_of(e_raw.at[1], eq_r.at[1])
     bytes_of(e_raw.at[2], eq_r.at[2])
@@ -218,15 +252,14 @@
         f_turn = jnp.where(j // NY == xh, away, 2 + away + away // 2)
         return jnp.maximum(e_turn, f_turn)
 
-    def products(stage, first, last):
-        @pl.loop(first, last)
-        def _(j):
+    def products(stage, first, count):
+        @pl.loop(0, count)
+        def _(i):
+            j = lax.rem(xh * NY + first + i, 2 * NY)
+
             @pl.when(stage_of(j) == stage)
             def _():
-                @pl.loop(0, nn // 256)
-                def _(n):
-                    cols = pl.ds(pl.multiple_of(n * 256, 256), 256)
-                    ang[:, cols] = ang[:, cols] + dot(f3[j], e3[j, :, cols])
+                ang[...] = ang[...] + dot(f3[j], e3[j])
 
     e_step(0, 0, 1)
     e_step(1, 0, 1)
@@ -246,68 +279,66 @@
     e_step(1, 1, 1)
     e_prep(1, lanes_c)
     e_prep(7, lanes_c)
-    e_step(0, 0, 2)
-    e_step(1, 0, 2)
     f_wait(0, 0, 1, clip_of(0, 3), mid, kc)
     f_wait(1, 0, 1, clip_of(0, 1), 0, mid)
+    f_prep(0, 1)
+    f_prep(0, 3)
     over = clip_of(1, 0)
     bytes_of(f_block(over, 0, cut), fx_r.at[2])
     f_send(0, 1, 0, over, 0, cut)
     f_send(1, 1, 0, over, 0, cut)
+    e_step(0, 0, 2)
+    e_step(1, 0, 2)
+    e_other(1)
+    e_other(7)
     bytes_of(f_block(over, cut, kc), fx_r.at[3])
     f_send(0, 1, 1, over, cut, mid)
     f_send(1, 1, 1, over, mid, kc)
     f_send(0, 1, 2, over, mid, kc)
     f_send(1, 1, 2, over, cut, mid)
-    send_w(1, 0)
-    f_prep(0, 1)
-    f_prep(0, 3)
+    products(1, 0, 4)
     e_step(0, 1, 2)
     e_step(1, 1, 2)
-    e_other(1)
-    e_other(7)
-    products(1, 0, 8)
+    products(1, 4, 4)
     e_prep(2, lanes_c)
     e_prep(6, lanes_c)
     f_wait(0, 0, 2, clip_of(0, 2), 0, mid)
     f_wait(1, 0, 2, clip_of(0, 2), mid, kc)
-    send_w(0, 2)
     f_prep(0, 2)
     f_prep(1, 0)
+    e_other(2)
+    e_other(6)
     e_step(0, 0, 3)
     e_step(1, 0, 3)
-    e_other(2)
-    e_other(6)
+    products(2, 0, 2)
     f_wait(0, 1, 0, clip_of(1, 3), 0, cut)
     f_wait(0, 1, 1, clip_of(1, 3), cut, mid)
     f_send(0, 1, 3, clip_of(1, 3), 0, mid)
     f_wait(1, 1, 0, clip_of(1, 1), 0, cut)
     f_wait(1, 1, 1, clip_of(1, 1), mid, kc)
     f_send(1, 1, 3, clip_of(1, 1), mid, kc)
-    products(2, 0, 4)
+    products(2, 2, 2)
     e_step(0, 1, 3)
     e_step(1, 1, 3)
-    products(2, 4, 8)
+    products(2, 4, 4)
     e_prep(3, lanes_c)
     e_prep(5, lanes_c)
     f_wait(0, 1, 2, clip_of(1, 3), mid, kc)
     f_wait(1, 1, 2, clip_of(1, 1), cut, mid)
-    send_w(1, 1)
-    send_w(1, 3)
     f_prep(1, 1)
     f_prep(1, 3)
     e_step(0, 0, 4)
+    e_other(3)
+    e_other(5)
+    products(3, 0, 4)
     e_step(1, 1, 4)
     e_prep(4, lanes_c)
-    e_other(3)
-    e_other(5)
-    products(3, 0, 8)
+    products(3, 4, 4)
     e_other(4)
     products(4, 0, 8)
     last_block = clip_of(1, 2)
     f_wait(0, 1, 3, last_block, 0, mid)
     f_wait(1, 1, 3, last_block, mid, kc)
-    send_w(1, 2)
     f_prep(1, 2)
 
     @pl.loop(0, nn // 256)
@@ -380,21 +411,17 @@
         w_t[t + 1, my_rows, :] = w_half
         for u, dy in clip_offsets:
             put(w_send.at[t + 1], w_t.at[t + 1, my_rows, :], w_s.at[t + 1], w_r.at[t + 1], (clip_of(u, dy), feat), False)
-    tr_ref[...] = w_own[...]
+    store_trained = pltpu.make_async_copy(w_own, tr_hbm, out_s.at[0])
+    store_trained.start()
 
     t = STEPS
     bytes_of(g_recv.at[0], w_r.at[t])
-    row = lax.broadcasted_iota(jnp.int32, (2 * 128, 128), 0)
-    col = lax.broadcasted_iota(jnp.int32, (2 * 128, 128), 1)
-    row_q = lax.broadcasted_iota(jnp.int32, (2 * 128, 1), 0) // 4 % 4
+    logits[...] = dot(w_t[t], phi[...]).astype(jnp.bfloat16)
 
     def chip_blocks(core):
-        pick = col == 8 * (row // 16) + 4 * core + row % 4
-        w = dot(pick.astype(jnp.float32).astype(jnp.bfloat16), w_t[t])
-        out = jnp.zeros((2 * 128, quarter), jnp.float32)
-        for q in range(4):
-            w_q = jnp.where(row_q == q, w, 0.0).astype(jnp.bfloat16)
-            out = out + dot(w_q, phi[:, q * quarter:(q + 1) * quarter])
+        out = dot(picks[core, 0], logits[:, 0:quarter])
+        for q in range(1, 4):
+            out = out + dot(picks[core, q], logits[:, q * quarter:(q + 1) * quarter])
         return out
 
     out = chip_blocks(1 - c).astype(jnp.bfloat16)
@@ -416,6 +443,10 @@
     acc = exchange(t, lambda pz, px: c_send.at[(t, *block_of(pz, px))], lambda: part[block_of(z, xl)])
     for q in range(4):
         sc_ref[:, q * quarter:(q + 1) * quarter] = acc[4 * q:4 * q + 4, :]
+    store_scores = pltpu.make_async_copy(sc_ref, sc_hbm, out_s.at[1])
+    store_scores.start()
+    store_trained.wait()
+    store_scores.wait()
 
     for copy in sends:
         copy.wait_send()
@@ -437,10 +468,17 @@
     scale = math.sqrt(2.0 / total_features)
     f32, b16 = jnp.float32, jnp.bfloat16
     dma = pltpu.SemaphoreType.DMA
-    vm = pl.BlockSpec(memory_space=pltpu.VMEM)
+    hbm = pl.BlockSpec(memory_space=pl.ANY)
     half, quarter = nn // 2, nn // 4
     steps = STEPS + 1
     scratch = [
+        pltpu.VMEM((ke, nn), f32),
+        pltpu.VMEM((kc, nf), f32),
+        pltpu.VMEM((nf // 128, 128), f32),
+        pltpu.VMEM((kw, nf), f32),
+        pltpu.VMEM((nn, kk), jnp.int32),
+        pltpu.VMEM((4, nn), f32),
+        pltpu.VMEM((2, 4, 256, 128), b16),
         pltpu.VMEM((kt, nn), f32),
         pltpu.VMEM((kt, nf), f32),
         pltpu.VMEM((3, ke, half), f32),
@@ -463,16 +501,18 @@
         pltpu.VMEM((kk, nf), f32),
         pltpu.VMEM((STEPS, kk, nf), b16),
         pltpu.VMEM((STEPS, 7, kw, nf), b16),
+        pltpu.VMEM((kk, nn), b16),
         dma((3,)), dma((3,)), dma((2, 2, 4)), dma((2, 2, 4)), dma((2, NZ)), dma((NZ,)),
         dma((4,)), dma((4,)), dma((2, 2, 4)), dma((2, 2, 4)),
         dma((steps,)), dma((steps,)), dma((steps,)), dma((steps,)), dma((steps,)), dma((steps,)),
         dma((STEPS,)), dma((STEPS,)), dma((STEPS,)), dma((STEPS,)), dma((STEPS,)), dma((STEPS,)),
+        dma((5,)), dma((2,)), pltpu.SemaphoreType.REGULAR((3,)),
     ]
     trained_t, scores_t = pl.pallas_call(
         functools.partial(kernel, scale),
         out_shape=(jax.ShapeDtypeStruct((kw, nf), f32), jax.ShapeDtypeStruct((4, nn), f32)),
-        in_specs=[vm] * 5,
-        out_specs=(vm, vm),
+        in_specs=[hbm] * 5,
+        out_specs=(hbm, hbm),
         scratch_shapes=scratch,
         compiler_params=pltpu.CompilerParams(
             collective_id=0, has_side_effects=True, vmem_limit_bytes=60 * 1024 * 1024),

time: 112 us -> 105 us (0.938)
  Pallas kernels: 109 us -> 102 us
    pallas_call x1, Pallas kernels: 109 us -> 102 us  [per_device(): pl.pallas_call(functools.partial(kernel, scale), out_shape=(jax.ShapeDtyp...]
where the time goes in v3:
time: 105 us
  Pallas kernels  102 us (97%)
  local copies, waits for them, and re-layouts  2.01 us (2%)
    pallas_call x1, Pallas kernels, per_device(): pl.pallas_call(functools.partial(kernel, scale), out_shape=(jax.ShapeDtyp...  102 us

profile of v3, /device:TPU:1, one launch (start us, length us, event | category | flops | bytes accessed | tf_op | source)
XLA Modules:
  0.0 105.2 jit_solution(16096834711888621617)
XLA Ops:
  0.6 102.5 %shard_map.68 = (f32[16,640]{1,0:T(8,128)}, f32[4,1024]{1,0:T(4,128)}) custom-call(f32[36,1024]{1,0:T(8,128)} %bitcast.5, f32[144,640]{1,0:T(8,128)} %f_hbm.1, f32[5,128]{1,0:T(8,128)} %bitcast.9, f32[16,640]{1,0:T(8,128)} %bitcast.6, s32[1024,128]{1,0:T(8,128)} %lab_hbm.1), custom_call_target="tpu_custom_call" | custom-call | tf_op jit(solution)/shard_map/pallas_call | solution.py:511
  103.1 0.0 copy-start
  103.1 1.4 %copy.9 = f32[640,16]{0,1:T(8,128)} copy(f32[640,16]{0,1:T(8,128)} %bitcast.7) | data formatting | bytes 81920
  104.6 0.0 copy-done
  104.6 0.6 copy.10
Async XLA Ops:
  103.1 1.4 %copy-start = (f32[4,1024]{1,0:T(4,128)S(1)}, f32[4,1024]{1,0:T(4,128)}, u32[]{:S(2)}) copy-start(f32[4,1024]{1,0:T(4,128)} %get-tuple-element.5) | copy-start | bytes 49156

commit v4 on v3

--- a/solution.py
+++ b/solution.py
@@ -15,20 +15,20 @@
 NZ = 8
 
 PI_A = 3.1416015625
-PI_B = -8.909031748771667e-06
-PI_C = 1.2154188766544394e-10
+PI_B = -8.90890987648163e-06
 SIN = (9.99999976e-01, -1.66666473e-01, 8.33289467e-03, -1.98005800e-04, 2.58984559e-06)
 
 
-def scaled_cos(x, scale):
-    q = jnp.round(x * (0.5 / math.pi))
-    w = ((0.5 * x - q * PI_A) - q * PI_B) - q * PI_C
+def scaled_cos_of_twice(h, scale):
+    q = jnp.round(h * (1.0 / math.pi))
+    w = (h - q * PI_A) - q * PI_B
     w2 = w * w
-    p = SIN[4]
+    root = math.sqrt(2.0 * scale)
+    p = root * SIN[4]
     for c in SIN[3::-1]:
-        p = p * w2 + c
+        p = p * w2 + root * c
     s = w * p
-    return scale - (2.0 * scale) * (s * s)
+    return scale - s * s
 
 
 def bytes_of(ref, sem):
@@ -38,8 +38,8 @@
 def kernel(
     scale,
     e_hbm, f_hbm, ph_hbm, w_hbm, lab_hbm,
-    tr_hbm, sc_hbm,
-    e_ref, f_ref, ph_ref, w_ref, lab_ref, sc_ref, picks,
+    tr_ref, sc_ref,
+    e_ref, f_ref, ph_ref, w_ref, lab_ref, picks,
     e_all, f_all, e_raw, e_two, f_rel,
     e3, f3, ang, phi, lab_t,
     w_own, w_send, w_t,
@@ -48,7 +48,7 @@
     eq_s, eq_r, er_s, er_r, ep_s, ep_r,
     fx_s, fx_r, fy_s, fy_r,
     w_s, w_r, c_s, c_r, l_s, l_r, r_s, r_r, rc_s, rc_r, g_s, g_r,
-    in_s, out_s, hello,
+    in_s, hello,
 ):
     loads = [
         pltpu.make_async_copy(src, dst, in_s.at[i])
@@ -163,9 +163,6 @@
         for direction in (0, 1):
             lo = lows[k ^ direction]
             f_send(direction, 0, k, clip, lo, lo + mid, f_ref.at[lo:lo + mid, :])
-    greeted(0)
-    greet(1)
-
     def join(own, oth):
         first = c == 0
         e_two[0:ke, :] = jnp.where(first, own, oth)
@@ -182,8 +179,8 @@
     e_all[e_rows(z, xl), lanes_c] = join(e_ref[:, lanes_c], e_raw[0])
     e_start(0, xl)
 
-    greeted(1)
-    greet(2)
+    greeted(0)
+    greet(1)
     for load in loads[3:]:
         load.wait()
     f_all[pl.ds(pl.multiple_of(clip * kc, 8), kc), :] = f_ref[...]
@@ -197,12 +194,9 @@
     qn = pl.multiple_of((2 * c + xl) * quarter, quarter)
     lab_t[...] = lab_ref[pl.ds(qn, quarter), :].astype(jnp.float32).T
     for b in range(nf // 128):
-        column = jnp.broadcast_to(ph_ref[b:b + 1, :], (128, 128)).T
+        column = jnp.broadcast_to(0.5 * ph_ref[b:b + 1, :], (128, 128)).T
         for n in range(nn // 128):
             ang[128 * b:128 * b + 128, 128 * n:128 * n + 128] = column
-    greeted(2)
-    for u, dy in clip_offsets:
-        send_w(u, dy)
 
     bytes_of(e_raw.at[1], eq_r.at[1])
     bytes_of(e_raw.at[2], eq_r.at[2])
@@ -221,7 +215,7 @@
 
     def e_prep(dz, lanes):
         z_ = lax.rem(z + dz, NZ)
-        x = e_all[pl.ds(pl.multiple_of(z_ * kc, 16), kc), lanes]
+        x = 0.5 * e_all[pl.ds(pl.multiple_of(z_ * kc, 16), kc), lanes]
         hi = x.astype(jnp.bfloat16)
         e3[z_, 0:kc, lanes] = hi
         e3[z_, kc:2 * kc, lanes] = (x - hi.astype(jnp.float32)).astype(jnp.bfloat16)
@@ -247,9 +241,10 @@
     def stage_of(j):
         up = lax.rem(j - z + NZ, NZ)
         e_turn = jnp.minimum(up, NZ - up)
+        e_turn = e_turn + e_turn // 4
         right = lax.rem(lax.rem(j, NY) - y + NY, NY)
         away = jnp.minimum(right, NY - right)
-        f_turn = jnp.where(j // NY == xh, away, 2 + away + away // 2)
+        f_turn = jnp.where(j // NY == xh, away, 2 + away)
         return jnp.maximum(e_turn, f_turn)
 
     def products(stage, first, count):
@@ -263,6 +258,8 @@
 
     e_step(0, 0, 1)
     e_step(1, 0, 1)
+    greeted(1)
+    greet(2)
     f_wait(0, 0, 0, clip_of(0, 3), 0, mid)
     f_send(0, 0, 2, clip_of(0, 3), 0, mid)
     f_wait(1, 0, 0, clip_of(0, 1), mid, kc)
@@ -271,6 +268,9 @@
     put(f_rel.at[cut:kc, :], f_block(clip_of(1, 0), cut, kc), fx_s.at[3], fx_r.at[3], x_near)
     bytes_of(f_rel.at[0:cut, :], fx_r.at[0])
     put(f_rel.at[0:cut, :], f_block(clip, 0, cut), fx_s.at[2], fx_r.at[2], x_cross)
+    greeted(2)
+    for u, dy in clip_offsets:
+        send_w(u, dy)
     e_prep(0, lanes_c)
     f_prep(0, 0)
     e_other(0)
@@ -331,23 +331,25 @@
     e_other(3)
     e_other(5)
     products(3, 0, 4)
+    products(3, 4, 4)
     e_step(1, 1, 4)
     e_prep(4, lanes_c)
-    products(3, 4, 4)
+    last_f = clip_of(1, 2)
+    last = lax.rem(z + 4, NZ)
+    f_wait(0, 1, 3, last_f, 0, mid)
+    f_wait(1, 1, 3, last_f, mid, kc)
+    f_prep(1, 2)
+
+    @pl.when(last_f != last)
+    def _():
+        ang[...] = ang[...] + dot(f3[last_f], e3[last_f])
+
     e_other(4)
-    products(4, 0, 8)
-    last_block = clip_of(1, 2)
-    f_wait(0, 1, 3, last_block, 0, mid)
-    f_wait(1, 1, 3, last_block, mid, kc)
-    f_prep(1, 2)
-
-    @pl.loop(0, nn // 256)
-    def _(n):
-        cols = pl.ds(pl.multiple_of(n * 256, 256), 256)
-        for m in range(nf // 128):
-            rows = slice(128 * m, 128 * m + 128)
-            x = ang[rows, cols] + dot(f3[last_block, rows, :], e3[last_block, :, cols])
-            phi[rows, cols] = scaled_cos(x, scale).astype(jnp.bfloat16)
+
+    for n in range(nn // 256):
+        cols = slice(256 * n, 256 * n + 256)
+        x = ang[:, cols] + dot(f3[last], e3[last, :, cols])
+        phi[:, cols] = scaled_cos_of_twice(x, scale).astype(jnp.bfloat16)
 
     my_block = pl.ds(pl.multiple_of(z * 16, 16), 16)
     my_lanes = pl.ds(pl.multiple_of(xl * quarter, quarter), quarter)
@@ -411,8 +413,7 @@
         w_t[t + 1, my_rows, :] = w_half
         for u, dy in clip_offsets:
             put(w_send.at[t + 1], w_t.at[t + 1, my_rows, :], w_s.at[t + 1], w_r.at[t + 1], (clip_of(u, dy), feat), False)
-    store_trained = pltpu.make_async_copy(w_own, tr_hbm, out_s.at[0])
-    store_trained.start()
+    tr_ref[...] = w_own[...]
 
     t = STEPS
     bytes_of(g_recv.at[0], w_r.at[t])
@@ -443,10 +444,6 @@
     acc = exchange(t, lambda pz, px: c_send.at[(t, *block_of(pz, px))], lambda: part[block_of(z, xl)])
     for q in range(4):
         sc_ref[:, q * quarter:(q + 1) * quarter] = acc[4 * q:4 * q + 4, :]
-    store_scores = pltpu.make_async_copy(sc_ref, sc_hbm, out_s.at[1])
-    store_scores.start()
-    store_trained.wait()
-    store_scores.wait()
 
     for copy in sends:
         copy.wait_send()
@@ -469,6 +466,7 @@
     f32, b16 = jnp.float32, jnp.bfloat16
     dma = pltpu.SemaphoreType.DMA
     hbm = pl.BlockSpec(memory_space=pl.ANY)
+    vmem = pl.BlockSpec(memory_space=pltpu.VMEM)
     half, quarter = nn // 2, nn // 4
     steps = STEPS + 1
     scratch = [
@@ -477,7 +475,6 @@
         pltpu.VMEM((nf // 128, 128), f32),
         pltpu.VMEM((kw, nf), f32),
         pltpu.VMEM((nn, kk), jnp.int32),
-        pltpu.VMEM((4, nn), f32),
         pltpu.VMEM((2, 4, 256, 128), b16),
         pltpu.VMEM((kt, nn), f32),
         pltpu.VMEM((kt, nf), f32),
@@ -506,13 +503,13 @@
         dma((4,)), dma((4,)), dma((2, 2, 4)), dma((2, 2, 4)),
         dma((steps,)), dma((steps,)), dma((steps,)), dma((steps,)), dma((steps,)), dma((steps,)),
         dma((STEPS,)), dma((STEPS,)), dma((STEPS,)), dma((STEPS,)), dma((STEPS,)), dma((STEPS,)),
-        dma((5,)), dma((2,)), pltpu.SemaphoreType.REGULAR((3,)),
+        dma((5,)), pltpu.SemaphoreType.REGULAR((3,)),
     ]
     trained_t, scores_t = pl.pallas_call(
         functools.partial(kernel, scale),
-        out_shape=(jax.ShapeDtypeStruct((kw, nf), f32), jax.ShapeDtypeStruct((4, nn), f32)),
+        out_shape=(pltpu.VMEM((kw, nf), f32), pltpu.VMEM((4, nn), f32)),
         in_specs=[hbm] * 5,
-        out_specs=(hbm, hbm),
+        out_specs=(vmem, vmem),
         scratch_shapes=scratch,
         compiler_params=pltpu.CompilerParams(
             collective_id=0, has_side_effects=True, vmem_limit_bytes=60 * 1024 * 1024),

time: 105 us -> 101 us (0.962)
  Pallas kernels: 102 us -> 99.1 us
    pallas_call x1, Pallas kernels: 102 us -> 99.1 us  [per_device(): pl.pallas_call(functools.partial(kernel, scale), out_shape=(pltpu.VMEM((k...]
where the time goes in v4:
time: 101 us
  Pallas kernels  99.1 us (98%)
  local copies, waits for them, and re-layouts  1.22 us (1%)
    pallas_call x1, Pallas kernels, per_device(): pl.pallas_call(functools.partial(kernel, scale), out_shape=(pltpu.VMEM((k...  99.1 us

profile of v4, /device:TPU:1, one launch (start us, length us, event | category | flops | bytes accessed | tf_op | source)
XLA Modules:
  0.0 101.0 jit_solution(16383511209976714238)
XLA Ops:
  0.6 99.1 %shard_map.68 = (f32[16,640]{1,0:T(8,128)S(1)}, f32[4,1024]{1,0:T(4,128)S(1)}) custom-call(f32[36,1024]{1,0:T(8,128)} %bitcast.7, f32[144,640]{1,0:T(8,128)} %f_hbm.1, f32[5,128]{1,0:T(8,128)} %bitcast.9, f32[16,640]{1,0:T(8,128)} %bitcast.8, s32[1024,128]{1,0:T(8,128)} %lab_hbm.1), custom_call_target="tpu_custom_call" | custom-call | tf_op jit(solution)/shard_map/pallas_call | solution.py:508
  99.8 0.6 copy.9
  100.4 0.6 copy.10

commit v5 on v4

--- a/solution.py
+++ b/solution.py
@@ -44,7 +44,7 @@
     e3, f3, ang, phi, lab_t,
     w_own, w_send, w_t,
     part, c_send, c_recv, l_send, l_recv, r_t,
-    grad, g_send, g_recv, logits,
+    grad, g_send, g_recv, logits, s_out, s_in, s_own, s_sum, s_recv,
     eq_s, eq_r, er_s, er_r, ep_s, ep_r,
     fx_s, fx_r, fy_s, fy_r,
     w_s, w_r, c_s, c_r, l_s, l_r, r_s, r_r, rc_s, rc_r, g_s, g_r,
@@ -95,9 +95,6 @@
     feat_offsets = [(dz, dx) for dz in (4, 3, 5, 2, 6, 1, 7, 0) for dx in (1, 0) if (dz, dx) != (0, 0)]
     clip_offsets = [(u, dy) for dy in (2, 1, 3, 0) for u in (1, 0) if (u, dy) != (0, 0)]
 
-    def slot_of(u, dy):
-        return u * NY + dy - 1
-
     barrier = pltpu.get_barrier_semaphore()
     neighbours = [partner, x_near, x_cross, diag, z_up, z_down, y_right, y_left]
     for peer in neighbours:
@@ -142,7 +139,7 @@
         return f_all.at[pl.ds(pl.multiple_of(clip_ * kc + lo, 8), hi - lo), :]
 
     def send_w(u, dy):
-        put(w_send.at[0], w_t.at[0, my_rows, :], w_s.at[0], w_r.at[0], (clip_of(u, dy), feat), False)
+        put(w_send.at[0], w_t.at[0, my_rows, :], w_s.at[0], w_r.at[0, 0], (clip_of(u, dy), feat), False)
 
     put(e_ref.at[:, lanes_o], e_raw.at[0], eq_s.at[0], eq_r.at[0], partner)
     put(e_ref.at[:, lanes_c], e_raw.at[1], eq_s.at[1], eq_r.at[1], x_near)
@@ -184,15 +181,17 @@
     for load in loads[3:]:
         load.wait()
     f_all[pl.ds(pl.multiple_of(clip * kc, 8), kc), :] = f_ref[...]
-    row = lax.broadcasted_iota(jnp.int32, (2 * 128, 128), 0)
-    col = lax.broadcasted_iota(jnp.int32, (2 * 128, 128), 1)
+    row = lax.broadcasted_iota(jnp.int32, (128, 64), 0)
+    col = lax.broadcasted_iota(jnp.int32, (128, 64), 1)
     for core in range(2):
         there = col == 8 * (row // 16) + 4 * core + row % 4
         for q in range(4):
             pick = there & (row // 4 % 4 == q)
             picks[core, q] = jnp.where(pick, 1.0, 0.0).astype(jnp.bfloat16)
-    qn = pl.multiple_of((2 * c + xl) * quarter, quarter)
-    lab_t[...] = lab_ref[pl.ds(qn, quarter), :].astype(jnp.float32).T
+    first = pl.multiple_of(c * half + (xl * 2 + z // 4) * (nn // 8), nn // 8)
+    lab = lab_ref[pl.ds(first, nn // 8), :].astype(jnp.float32).T
+    lab_t[0] = lab[0:4 * kw, :]
+    lab_t[1] = lab[4 * kw:8 * kw, :]
     for b in range(nf // 128):
         column = jnp.broadcast_to(0.5 * ph_ref[b:b + 1, :], (128, 128)).T
         for n in range(nn // 128):
@@ -351,97 +350,147 @@
         x = ang[:, cols] + dot(f3[last], e3[last, :, cols])
         phi[:, cols] = scaled_cos_of_twice(x, scale).astype(jnp.bfloat16)
 
-    my_block = pl.ds(pl.multiple_of(z * 16, 16), 16)
-    my_lanes = pl.ds(pl.multiple_of(xl * quarter, quarter), quarter)
-
-    def exchange(t, source, own):
+    hk = w_t.shape[1] // 2
+    block = nn // 8
+    chains = range(2)
+
+    def chain_rows(h):
+        return slice(h * hk, (h + 1) * hk)
+
+    def block_rows(z_):
+        return pl.ds(pl.multiple_of(lax.rem(z_, 4) * 16, 16), 16)
+
+    def block_lanes(z_, xl_, core=None):
+        lane = (xl_ * 2 + z_ // 4) * block
+        if core is not None:
+            lane = lane + core * half
+        return pl.ds(pl.multiple_of(lane, block), block)
+
+    nt = functools.partial(
+        lax.dot_general, dimension_numbers=(((1,), (1,)), ((), ())), preferred_element_type=jnp.float32)
+
+    def wait_w(t, h):
+        for own, count in ((True, 3), (False, 4)):
+            @pl.when((xh == h) == own)
+            def _():
+                bytes_of(g_recv.at[0, 0:count], w_r.at[t, h])
+
+    def start_logits(t, h):
+        w = w_t[t, chain_rows(h), :]
+        c_send[t, h] = dot(w, phi[:, lanes_o]).astype(jnp.bfloat16)
+        put(c_send.at[t, h], c_recv.at[t, h], c_s.at[t, h], c_r.at[t, h], partner)
+        part[h] = dot(w, phi[:, lanes_c])
+
+    def share_logits(t, h):
+        bytes_of(c_recv.at[t, h], c_r.at[t, h])
+        total = part[h] + c_recv[t, h].astype(jnp.float32)
+        part[h] = total
+        l_send[t, h] = total.astype(jnp.bfloat16)
         for dz, dx in feat_offsets:
             pz, px = feat_peer(dz, dx)
-            put(source(pz, px), l_recv.at[t, dx * NZ + dz - 1], l_s.at[t], l_r.at[t], (clip, feat_of(pz, px, c)), False)
-        acc = own()
-        bytes_of(l_recv.at[t], l_r.at[t])
-        for i in range(2 * NZ - 1):
-            acc = acc + l_recv[t, i].astype(jnp.float32)
-        return acc
-
-    def summed_logits(t):
-        w = w_t[t]
-        c_send[t] = dot(w, phi[:, lanes_o]).astype(jnp.bfloat16)
-        put(c_send.at[t], c_recv.at[t], c_s.at[t], c_r.at[t], partner)
-        part[...] = dot(w, phi[:, lanes_c])
-        bytes_of(c_recv.at[t], c_r.at[t])
-        total = part[...] + c_recv[t].astype(jnp.float32)
-        part[...] = total
-        l_send[t] = total.astype(jnp.bfloat16)
-
-        def source(pz, px):
-            return l_send.at[t, pl.ds(pl.multiple_of(pz * 16, 16), 16), pl.ds(pl.multiple_of(px * quarter, quarter), quarter)]
-
-        return exchange(t, source, lambda: part[my_block, my_lanes])
-
-    nt = (((1,), (1,)), ((), ()))
-    full_lanes = pl.ds(pl.multiple_of(c * half + xl * quarter, quarter), quarter)
-
+            put(l_send.at[t, h, block_rows(pz), block_lanes(pz, px)], l_recv.at[t, h, dx * NZ + dz - 1],
+                l_s.at[t, h], l_r.at[t, h], (clip, feat_of(pz, px, c)), False)
+
+    bytes_of(g_recv.at[0], w_r.at[0, 0])
+    for h in chains:
+        start_logits(0, h)
     for t in range(STEPS):
-        bytes_of(g_recv.at[0], w_r.at[t])
-        acc = summed_logits(t)
-        residual = (jax.nn.sigmoid(acc) - lab_t[my_block, :]).astype(jnp.bfloat16)
-        r_t[t, my_block, full_lanes] = residual
-        mine_r = r_t.at[t, my_block, full_lanes]
-        for dz, dx in feat_offsets:
-            pz, px = feat_peer(dz, dx)
-            put(mine_r, mine_r, r_s.at[t], r_r.at[t], (clip, feat_of(pz, px, c)), False)
-        bytes_of(l_recv.at[t], r_r.at[t])
-        half_r = r_t.at[t, :, lanes_c]
-        put(half_r, half_r, rc_s.at[t], rc_r.at[t], partner)
-        grad[...] = lax.dot_general(r_t[t, :, lanes_c], phi[:, lanes_c], nt, preferred_element_type=jnp.float32)
-        bytes_of(r_t.at[t, :, lanes_o], rc_r.at[t])
-        total = grad[...] + lax.dot_general(r_t[t, :, lanes_o], phi[:, lanes_o], nt, preferred_element_type=jnp.float32)
-        grad[...] = total
-        g_send[t] = total.astype(jnp.bfloat16)
-        for u, dy in clip_offsets:
-            j = clip_of(u, dy)
-            put(g_send.at[t, pl.ds(pl.multiple_of(j * kw, kw), kw), :], g_recv.at[t, slot_of(u, dy)], g_s.at[t], g_r.at[t], (j, feat), False)
-        g = grad[my_rows, :]
-        bytes_of(g_recv.at[t], g_r.at[t])
-        for i in range(7):
-            g = g + g_recv[t, i].astype(jnp.float32)
-        w_new = w_own[...] - 0.25 * g
-        w_own[...] = w_new
-        w_half = w_new.astype(jnp.bfloat16)
-        w_send[t + 1] = w_half
-        w_t[t + 1, my_rows, :] = w_half
-        for u, dy in clip_offsets:
-            put(w_send.at[t + 1], w_t.at[t + 1, my_rows, :], w_s.at[t + 1], w_r.at[t + 1], (clip_of(u, dy), feat), False)
+        for h in chains:
+            if t > 0:
+                wait_w(t, h)
+                start_logits(t, h)
+            share_logits(t, h)
+        for h in chains:
+            acc = part[h, block_rows(z), block_lanes(z, xl)]
+            bytes_of(l_recv.at[t, h], l_r.at[t, h])
+            for i in range(2 * NZ - 1):
+                acc = acc + l_recv[t, h, i].astype(jnp.float32)
+            labels = lab_t[h, block_rows(z), :]
+            r_t[t, h, block_rows(z), block_lanes(z, xl, c)] = (jax.nn.sigmoid(acc) - labels).astype(jnp.bfloat16)
+            mine_r = r_t.at[t, h, block_rows(z), block_lanes(z, xl, c)]
+            for dz, dx in feat_offsets:
+                pz, px = feat_peer(dz, dx)
+                put(mine_r, mine_r, r_s.at[t, h], r_r.at[t, h], (clip, feat_of(pz, px, c)), False)
+        for h in chains:
+            bytes_of(l_recv.at[t, h], r_r.at[t, h])
+            half_r = r_t.at[t, h, :, lanes_c]
+            put(half_r, half_r, rc_s.at[t, h], rc_r.at[t, h], partner)
+            grad[h] = nt(r_t[t, h, :, lanes_c], phi[:, lanes_c])
+            bytes_of(r_t.at[t, h, :, lanes_o], rc_r.at[t, h])
+            total = grad[h] + nt(r_t[t, h, :, lanes_o], phi[:, lanes_o])
+            grad[h] = total
+            g_send[t, h] = total.astype(jnp.bfloat16)
+
+            def send_g(dy, slot):
+                yo = lax.rem(y + dy, NY)
+                put(g_send.at[t, h, pl.ds(pl.multiple_of(yo * kw, kw), kw), :], g_recv.at[t, slot],
+                    g_s.at[t, h], g_r.at[t], (h * NY + yo, feat), False)
+
+            slot = jnp.where(xh == h, -1, 3)
+            for dy in (2, 1, 3):
+                send_g(dy, slot + dy)
+
+            @pl.when(xh != h)
+            def _():
+                send_g(0, 3)
+        for h in chains:
+            @pl.when(xh == h)
+            def _():
+                g = grad[h, pl.ds(pl.multiple_of(y * kw, kw), kw), :]
+                bytes_of(g_recv.at[t], g_r.at[t])
+                for i in range(7):
+                    g = g + g_recv[t, i].astype(jnp.float32)
+                w_new = w_own[...] - 0.25 * g
+                w_own[...] = w_new
+                w_half = w_new.astype(jnp.bfloat16)
+                w_send[t + 1] = w_half
+                w_t[t + 1, my_rows, :] = w_half
+                for u, dy in clip_offsets:
+                    put(w_send.at[t + 1], w_t.at[t + 1, my_rows, :], w_s.at[t + 1], w_r.at[t + 1, h],
+                        (clip_of(u, dy), feat), False)
     tr_ref[...] = w_own[...]
 
     t = STEPS
-    bytes_of(g_recv.at[0], w_r.at[t])
-    logits[...] = dot(w_t[t], phi[...]).astype(jnp.bfloat16)
-
-    def chip_blocks(core):
-        out = dot(picks[core, 0], logits[:, 0:quarter])
+
+    def chip_blocks(h, core):
+        out = dot(picks[core, 0], logits[h, :, 0:quarter])
         for q in range(1, 4):
-            out = out + dot(picks[core, q], logits[:, q * quarter:(q + 1) * quarter])
+            out = out + dot(picks[core, q], logits[h, :, q * quarter:(q + 1) * quarter])
         return out
 
-    out = chip_blocks(1 - c).astype(jnp.bfloat16)
-    l_send[t, :, 0:quarter] = out[0:128, :]
-    l_send[t, :, quarter:half] = out[128:256, :]
-    put(l_send.at[t], c_recv.at[t], c_s.at[t], c_r.at[t], partner)
-    out = chip_blocks(c)
-    bytes_of(c_recv.at[t], c_r.at[t])
-    for h in range(2):
-        lanes = slice(h * quarter, (h + 1) * quarter)
-        total = out[128 * h:128 * h + 128, :] + c_recv[t, :, lanes].astype(jnp.float32)
-        part[:, lanes] = total
-        c_send[t, :, lanes] = total.astype(jnp.bfloat16)
-
-    def block_of(z_, xl_):
-        i = 2 * z_ + xl_
-        return pl.ds(pl.multiple_of(lax.rem(i, 8) * 16, 16), 16), pl.ds(pl.multiple_of(i // 8 * quarter, quarter), quarter)
-
-    acc = exchange(t, lambda pz, px: c_send.at[(t, *block_of(pz, px))], lambda: part[block_of(z, xl)])
+    def chip_rows(z_, xl_):
+        return pl.ds(pl.multiple_of((2 * lax.rem(z_, 4) + xl_) * 16, 16), 16)
+
+    zh = z // 4
+    for h in chains:
+        wait_w(t, h)
+        logits[h] = dot(w_t[t, chain_rows(h), :], phi[...]).astype(jnp.bfloat16)
+        s_out[h] = chip_blocks(h, 1 - c).astype(jnp.bfloat16)
+        put(s_out.at[h], s_in.at[h], c_s.at[t, h], c_r.at[t, h], partner)
+        s_own[h] = chip_blocks(h, c)
+        bytes_of(s_in.at[h], c_r.at[t, h])
+        total = s_own[h] + s_in[h].astype(jnp.float32)
+        s_own[h] = total
+        s_sum[h] = total.astype(jnp.bfloat16)
+
+        def send_s(dz, dx, slot):
+            pz = h * 4 + lax.rem(z + dz, 4)
+            px = 1 - xl if dx else xl
+            put(s_sum.at[h, chip_rows(pz, px), :], s_recv.at[slot], l_s.at[t, h], l_r.at[t, 0], (clip, feat_of(pz, px, c)), False)
+
+        slot = jnp.where(zh == h, -1, 7)
+        for dz in (2, 1, 3, 0):
+            for dx in (1, 0):
+                if (dz, dx) != (0, 0):
+                    send_s(dz, dx, slot + dx * 4 + dz)
+
+        @pl.when(zh != h)
+        def _():
+            send_s(0, 0, 7)
+    acc = s_own[zh, chip_rows(z, xl), :]
+    bytes_of(s_recv, l_r.at[t, 0])
+    for i in range(2 * NZ - 1):
+        acc = acc + s_recv[i].astype(jnp.float32)
     for q in range(4):
         sc_ref[:, q * quarter:(q + 1) * quarter] = acc[4 * q:4 * q + 4, :]
 
@@ -449,10 +498,19 @@
         copy.wait_send()
     for t in range(STEPS + 1):
         bytes_of(g_recv.at[0], w_s.at[t])
-        bytes_of(l_recv.at[0], l_s.at[t])
-    for t in range(STEPS):
-        bytes_of(l_recv.at[0], r_s.at[t])
-        bytes_of(g_recv.at[0], g_s.at[t])
+    for h in chains:
+        for t in range(STEPS):
+            bytes_of(l_recv.at[0, 0], l_s.at[t, h])
+            bytes_of(l_recv.at[0, 0], r_s.at[t, h])
+        for own, count in ((True, 3), (False, 4)):
+            @pl.when((xh == h) == own)
+            def _():
+                for t in range(STEPS):
+                    bytes_of(g_recv.at[0, 0:count], g_s.at[t, h])
+        for own, count in ((True, 7), (False, 8)):
+            @pl.when((zh == h) == own)
+            def _():
+                bytes_of(s_recv.at[0:count], l_s.at[STEPS, h])
 
 
 def per_device(embeds, frequencies, phases, weights, labels):
@@ -475,7 +533,7 @@
         pltpu.VMEM((nf // 128, 128), f32),
         pltpu.VMEM((kw, nf), f32),
         pltpu.VMEM((nn, kk), jnp.int32),
-        pltpu.VMEM((2, 4, 256, 128), b16),
+        pltpu.VMEM((2, 4, 128, 64), b16),
         pltpu.VMEM((kt, nn), f32),
         pltpu.VMEM((kt, nf), f32),
         pltpu.VMEM((3, ke, half), f32),
@@ -485,24 +543,29 @@
         pltpu.VMEM((8, nf, 3 * kc), b16),
         pltpu.VMEM((nf, nn), f32),
         pltpu.VMEM((nf, nn), b16),
-        pltpu.VMEM((kk, quarter), f32),
+        pltpu.VMEM((2, kk // 2, nn // 8), f32),
         pltpu.VMEM((kw, nf), f32),
         pltpu.VMEM((steps, kw, nf), b16),
         pltpu.VMEM((steps, kk, nf), b16),
-        pltpu.VMEM((kk, half), f32),
-        pltpu.VMEM((steps, kk, half), b16),
-        pltpu.VMEM((steps, kk, half), b16),
-        pltpu.VMEM((steps, kk, half), b16),
-        pltpu.VMEM((steps, 2 * NZ - 1, 16, quarter), b16),
-        pltpu.VMEM((STEPS, kk, nn), b16),
-        pltpu.VMEM((kk, nf), f32),
-        pltpu.VMEM((STEPS, kk, nf), b16),
+        pltpu.VMEM((2, kk // 2, half), f32),
+        pltpu.VMEM((STEPS, 2, kk // 2, half), b16),
+        pltpu.VMEM((STEPS, 2, kk // 2, half), b16),
+        pltpu.VMEM((STEPS, 2, kk // 2, half), b16),
+        pltpu.VMEM((STEPS, 2, 2 * NZ - 1, 16, nn // 8), b16),
+        pltpu.VMEM((STEPS, 2, kk // 2, nn), b16),
+        pltpu.VMEM((2, kk // 2, nf), f32),
+        pltpu.VMEM((STEPS, 2, kk // 2, nf), b16),
         pltpu.VMEM((STEPS, 7, kw, nf), b16),
-        pltpu.VMEM((kk, nn), b16),
+        pltpu.VMEM((2, kk // 2, nn), b16),
+        pltpu.VMEM((2, 128, quarter), b16),
+        pltpu.VMEM((2, 128, quarter), b16),
+        pltpu.VMEM((2, 128, quarter), f32),
+        pltpu.VMEM((2, 128, quarter), b16),
+        pltpu.VMEM((2 * NZ - 1, 16, quarter), b16),
         dma((3,)), dma((3,)), dma((2, 2, 4)), dma((2, 2, 4)), dma((2, NZ)), dma((NZ,)),
         dma((4,)), dma((4,)), dma((2, 2, 4)), dma((2, 2, 4)),
-        dma((steps,)), dma((steps,)), dma((steps,)), dma((steps,)), dma((steps,)), dma((steps,)),
-        dma((STEPS,)), dma((STEPS,)), dma((STEPS,)), dma((STEPS,)), dma((STEPS,)), dma((STEPS,)),
+        dma((steps,)), dma((steps, 2)), dma((steps, 2)), dma((steps, 2)), dma((steps, 2)), dma((steps, 2)),
+        dma((STEPS, 2)), dma((STEPS, 2)), dma((STEPS, 2)), dma((STEPS, 2)), dma((STEPS, 2)), dma((STEPS,)),
         dma((5,)), pltpu.SemaphoreType.REGULAR((3,)),
     ]
     trained_t, scores_t = pl.pallas_call(

time: 101 us -> 97.2 us (0.962)
  Pallas kernels: 99.1 us -> 95.2 us
    pallas_call x1, Pallas kernels: 99.1 us -> 95.2 us  [per_device(): pl.pallas_call(functools.partial(kernel, scale), out_shape=(pltpu.VMEM((k...]
where the time goes in v5:
time: 97.2 us; the launch traced here: 97.1 us
  Pallas kernels  95.2 us (98%)
  local copies, waits for them, and re-layouts  1.22 us (1%)
    pallas_call x1, Pallas kernels, per_device(): pl.pallas_call(functools.partial(kernel, scale), out_shape=(pltpu.VMEM((k...  95.2 us

profile of v5, /device:TPU:1, one launch (start us, length us, event | category | flops | bytes accessed | tf_op | source)
XLA Modules:
  0.0 97.1 jit_solution(15806337955488140570)
XLA Ops:
  0.6 95.2 %shard_map.68 = (f32[16,640]{1,0:T(8,128)S(1)}, f32[4,1024]{1,0:T(4,128)S(1)}) custom-call(f32[36,1024]{1,0:T(8,128)} %bitcast.7, f32[144,640]{1,0:T(8,128)} %f_hbm.1, f32[5,128]{1,0:T(8,128)} %bitcast.9, f32[16,640]{1,0:T(8,128)} %bitcast.8, s32[1024,128]{1,0:T(8,128)} %lab_hbm.1), custom_call_target="tpu_custom_call" | custom-call | tf_op jit(solution)/shard_map/pallas_call | solution.py:571
  95.9 0.6 copy.9
  96.5 0.6 copy.10

commit v6 on v5

--- a/solution.py
+++ b/solution.py
@@ -135,6 +135,10 @@
     def e_piece(z_, xl_):
         return e_all.at[e_rows(z_, xl_), lanes_c]
 
+    def e_far_piece(z_, xl_, direction):
+        lane = pl.multiple_of(c * half + direction * quarter, quarter)
+        return e_all.at[e_rows(z_, xl_), pl.ds(lane, quarter)]
+
     def f_block(clip_, lo, hi):
         return f_all.at[pl.ds(pl.multiple_of(clip_ * kc + lo, 8), hi - lo), :]
 
@@ -208,9 +212,16 @@
         xl_ = (1 - xl) if o else xl
         piece = e_piece(z_, xl_)
         bytes_of(piece, er_r.at[direction, o, s - 1])
-        if s < 3 or (s == 3 and o == direction):
-            put(piece, piece, er_s.at[direction, o, s], er_r.at[direction, o, s], z_up if direction == 0 else z_down)
+        on = piece if s < 3 else e_far_piece(z_, xl_, direction)
+        put(on, on, er_s.at[direction, o, s], er_r.at[direction, o, s], z_up if direction == 0 else z_down)
         put(piece, piece, ep_s.at[o, dz], ep_r.at[dz], partner)
+
+    def e_far(direction, o):
+        z_ = lax.rem(z + 4, NZ)
+        xl_ = (1 - xl) if o else xl
+        piece = e_far_piece(z_, xl_, direction)
+        bytes_of(piece, er_r.at[direction, o, 3])
+        put(piece, piece, ep_s.at[o, 4 + 4 * direction], ep_r.at[4], partner)
 
     def e_prep(dz, lanes):
         z_ = lax.rem(z + dz, NZ)
@@ -237,14 +248,18 @@
 
     dot = functools.partial(jnp.dot, preferred_element_type=jnp.float32)
 
+    LAST = 9
+    far = lax.rem(z + 4, NZ)
+    beside = jnp.where(far == clip_of(1, 2), clip_of(1, 1), clip_of(1, 2))
+
     def stage_of(j):
         up = lax.rem(j - z + NZ, NZ)
         e_turn = jnp.minimum(up, NZ - up)
-        e_turn = e_turn + e_turn // 4
+        e_turn = e_turn + e_turn // 3
         right = lax.rem(lax.rem(j, NY) - y + NY, NY)
         away = jnp.minimum(right, NY - right)
         f_turn = jnp.where(j // NY == xh, away, 2 + away)
-        return jnp.maximum(e_turn, f_turn)
+        return jnp.where(j == beside, LAST, jnp.maximum(e_turn, f_turn))
 
     def products(stage, first, count):
         @pl.loop(0, count)
@@ -267,9 +282,6 @@
     put(f_rel.at[cut:kc, :], f_block(clip_of(1, 0), cut, kc), fx_s.at[3], fx_r.at[3], x_near)
     bytes_of(f_rel.at[0:cut, :], fx_r.at[0])
     put(f_rel.at[0:cut, :], f_block(clip, 0, cut), fx_s.at[2], fx_r.at[2], x_cross)
-    greeted(2)
-    for u, dy in clip_offsets:
-        send_w(u, dy)
     e_prep(0, lanes_c)
     f_prep(0, 0)
     e_other(0)
@@ -316,38 +328,36 @@
     f_wait(1, 1, 0, clip_of(1, 1), 0, cut)
     f_wait(1, 1, 1, clip_of(1, 1), mid, kc)
     f_send(1, 1, 3, clip_of(1, 1), mid, kc)
-    products(2, 2, 2)
+    greeted(2)
+    for u, dy in clip_offsets:
+        send_w(u, dy)
+    products(2, 2, 6)
     e_step(0, 1, 3)
     e_step(1, 1, 3)
-    products(2, 4, 4)
-    e_prep(3, lanes_c)
-    e_prep(5, lanes_c)
     f_wait(0, 1, 2, clip_of(1, 3), mid, kc)
     f_wait(1, 1, 2, clip_of(1, 1), cut, mid)
     f_prep(1, 1)
     f_prep(1, 3)
-    e_step(0, 0, 4)
+    products(3, 4, 4)
+    e_prep(3, lanes_c)
+    e_prep(5, lanes_c)
+    e_far(0, 0)
+    e_far(1, 0)
     e_other(3)
     e_other(5)
-    products(3, 0, 4)
-    products(3, 4, 4)
-    e_step(1, 1, 4)
+    products(4, 0, 4)
+    e_far(0, 1)
+    e_far(1, 1)
     e_prep(4, lanes_c)
-    last_f = clip_of(1, 2)
-    last = lax.rem(z + 4, NZ)
-    f_wait(0, 1, 3, last_f, 0, mid)
-    f_wait(1, 1, 3, last_f, mid, kc)
+    products(4, 4, 4)
+    f_wait(0, 1, 3, clip_of(1, 2), 0, mid)
+    f_wait(1, 1, 3, clip_of(1, 2), mid, kc)
     f_prep(1, 2)
-
-    @pl.when(last_f != last)
-    def _():
-        ang[...] = ang[...] + dot(f3[last_f], e3[last_f])
-
     e_other(4)
 
     for n in range(nn // 256):
         cols = slice(256 * n, 256 * n + 256)
-        x = ang[:, cols] + dot(f3[last], e3[last, :, cols])
+        x = ang[:, cols] + dot(f3[beside], e3[beside, :, cols]) + dot(f3[far], e3[far, :, cols])
         phi[:, cols] = scaled_cos_of_twice(x, scale).astype(jnp.bfloat16)
 
     hk = w_t.shape[1] // 2
@@ -392,8 +402,13 @@
                 l_s.at[t, h], l_r.at[t, h], (clip, feat_of(pz, px, c)), False)
 
     bytes_of(g_recv.at[0], w_r.at[0, 0])
+    out = dot(w_t[0], phi[:, lanes_o]).astype(jnp.bfloat16)
     for h in chains:
-        start_logits(0, h)
+        c_send[0, h] = out[chain_rows(h), :]
+        put(c_send.at[0, h], c_recv.at[0, h], c_s.at[0, h], c_r.at[0, h], partner)
+    out = dot(w_t[0], phi[:, lanes_c])
+    for h in chains:
+        part[h] = out[chain_rows(h), :]
     for t in range(STEPS):
         for h in chains:
             if t > 0:
@@ -562,7 +577,7 @@
         pltpu.VMEM((2, 128, quarter), f32),
         pltpu.VMEM((2, 128, quarter), b16),
         pltpu.VMEM((2 * NZ - 1, 16, quarter), b16),
-        dma((3,)), dma((3,)), dma((2, 2, 4)), dma((2, 2, 4)), dma((2, NZ)), dma((NZ,)),
+        dma((3,)), dma((3,)), dma((2, 2, 4)), dma((2, 2, 4)), dma((2, NZ + 1)), dma((NZ,)),
         dma((4,)), dma((4,)), dma((2, 2, 4)), dma((2, 2, 4)),
         dma((steps,)), dma((steps, 2)), dma((steps, 2)), dma((steps, 2)), dma((steps, 2)), dma((steps, 2)),
         dma((STEPS, 2)), dma((STEPS, 2)), dma((STEPS, 2)), dma((STEPS, 2)), dma((STEPS, 2)), dma((STEPS,)),

time: 97.2 us -> 95.6 us (0.984)
  Pallas kernels: 95.2 us -> 93.6 us
    pallas_call x1, Pallas kernels: 95.2 us -> 93.6 us  [per_device(): pl.pallas_call(functools.partial(kernel, scale), out_shape=(pltpu.VMEM((k...]
where the time goes in v6:
time: 95.6 us; the launch traced here: 95.5 us
  Pallas kernels  93.6 us (98%)
  local copies, waits for them, and re-layouts  1.22 us (1%)
    pallas_call x1, Pallas kernels, per_device(): pl.pallas_call(functools.partial(kernel, scale), out_shape=(pltpu.VMEM((k...  93.6 us

profile of v6, /device:TPU:1, one launch (start us, length us, event | category | flops | bytes accessed | tf_op | source)
XLA Modules:
  0.0 95.5 jit_solution(2593091598355587837)
XLA Ops:
  0.6 93.6 %shard_map.68 = (f32[16,640]{1,0:T(8,128)S(1)}, f32[4,1024]{1,0:T(4,128)S(1)}) custom-call(f32[36,1024]{1,0:T(8,128)} %bitcast.7, f32[144,640]{1,0:T(8,128)} %f_hbm.1, f32[5,128]{1,0:T(8,128)} %bitcast.9, f32[16,640]{1,0:T(8,128)} %bitcast.8, s32[1024,128]{1,0:T(8,128)} %lab_hbm.1), custom_call_target="tpu_custom_call" | custom-call | tf_op jit(solution)/shard_map/pallas_call | solution.py:586
  94.3 0.6 copy.9
  94.9 0.6 copy.10

commit v7 on v6

--- a/solution.py
+++ b/solution.py
@@ -100,7 +100,11 @@
     for peer in neighbours:
         pl.semaphore_signal(barrier, inc=1, device_id=peer, device_id_type=MESH)
 
-    my_rows = pl.ds(pl.multiple_of(clip * kw, kw), kw)
+    def local_block(clip_):
+        return clip_ // NY * 2 + lax.rem(clip_, 2)
+
+    my_chain = y // 2
+    my_rows = pl.ds(pl.multiple_of(my_chain * 4 * kw + local_block(clip) * kw, kw), kw)
     for load in loads[0:3]:
         load.wait()
     w_own[...] = w_ref[...]
@@ -194,8 +198,9 @@
             picks[core, q] = jnp.where(pick, 1.0, 0.0).astype(jnp.bfloat16)
     first = pl.multiple_of(c * half + (xl * 2 + z // 4) * (nn // 8), nn // 8)
     lab = lab_ref[pl.ds(first, nn // 8), :].astype(jnp.float32).T
-    lab_t[0] = lab[0:4 * kw, :]
-    lab_t[1] = lab[4 * kw:8 * kw, :]
+    for h in range(2):
+        for i, of in enumerate((2 * h, 2 * h + 1, NY + 2 * h, NY + 2 * h + 1)):
+            lab_t[h, i * kw:(i + 1) * kw, :] = lab[of * kw:(of + 1) * kw, :]
     for b in range(nf // 128):
         column = jnp.broadcast_to(0.5 * ph_ref[b:b + 1, :], (128, 128)).T
         for n in range(nn // 128):
@@ -381,7 +386,7 @@
 
     def wait_w(t, h):
         for own, count in ((True, 3), (False, 4)):
-            @pl.when((xh == h) == own)
+            @pl.when((my_chain == h) == own)
             def _():
                 bytes_of(g_recv.at[0, 0:count], w_r.at[t, h])
 
@@ -436,22 +441,22 @@
             grad[h] = total
             g_send[t, h] = total.astype(jnp.bfloat16)
 
-            def send_g(dy, slot):
-                yo = lax.rem(y + dy, NY)
-                put(g_send.at[t, h, pl.ds(pl.multiple_of(yo * kw, kw), kw), :], g_recv.at[t, slot],
-                    g_s.at[t, h], g_r.at[t], (h * NY + yo, feat), False)
-
-            slot = jnp.where(xh == h, -1, 3)
-            for dy in (2, 1, 3):
-                send_g(dy, slot + dy)
-
-            @pl.when(xh != h)
+            def send_g(u, yo):
+                to = clip_of(u, yo - y + NY)
+                rows = pl.ds(pl.multiple_of(local_block(to) * kw, kw), kw)
+                slot = u * NY + lax.rem(yo - y + NY, NY) - 1
+                put(g_send.at[t, h, rows, :], g_recv.at[t, slot], g_s.at[t, h], g_r.at[t], (to, feat), False)
+
+            for yo in (2 * h, 2 * h + 1):
+                send_g(1, yo)
+
+                @pl.when(yo != y)
+                def _():
+                    send_g(0, yo)
+        for h in chains:
+            @pl.when(my_chain == h)
             def _():
-                send_g(0, 3)
-        for h in chains:
-            @pl.when(xh == h)
-            def _():
-                g = grad[h, pl.ds(pl.multiple_of(y * kw, kw), kw), :]
+                g = grad[h, pl.ds(pl.multiple_of(local_block(clip) * kw, kw), kw), :]
                 bytes_of(g_recv.at[t], g_r.at[t])
                 for i in range(7):
                     g = g + g_recv[t, i].astype(jnp.float32)
@@ -474,9 +479,9 @@
         return out
 
     def chip_rows(z_, xl_):
-        return pl.ds(pl.multiple_of((2 * lax.rem(z_, 4) + xl_) * 16, 16), 16)
-
-    zh = z // 4
+        return pl.ds(pl.multiple_of((2 * local_block(z_) + xl_) * 16, 16), 16)
+
+    z_chain = lax.rem(z, 4) // 2
     for h in chains:
         wait_w(t, h)
         logits[h] = dot(w_t[t, chain_rows(h), :], phi[...]).astype(jnp.bfloat16)
@@ -488,21 +493,18 @@
         s_own[h] = total
         s_sum[h] = total.astype(jnp.bfloat16)
 
-        def send_s(dz, dx, slot):
-            pz = h * 4 + lax.rem(z + dz, 4)
+        def send_s(pz, dx):
             px = 1 - xl if dx else xl
+            slot = dx * NZ + lax.rem(pz - z + NZ, NZ) - 1
             put(s_sum.at[h, chip_rows(pz, px), :], s_recv.at[slot], l_s.at[t, h], l_r.at[t, 0], (clip, feat_of(pz, px, c)), False)
 
-        slot = jnp.where(zh == h, -1, 7)
-        for dz in (2, 1, 3, 0):
-            for dx in (1, 0):
-                if (dz, dx) != (0, 0):
-                    send_s(dz, dx, slot + dx * 4 + dz)
-
-        @pl.when(zh != h)
-        def _():
-            send_s(0, 0, 7)
-    acc = s_own[zh, chip_rows(z, xl), :]
+        for pz in (2 * h, 2 * h + 1, NY + 2 * h, NY + 2 * h + 1):
+            send_s(pz, 1)
+
+            @pl.when(pz != z)
+            def _():
+                send_s(pz, 0)
+    acc = s_own[z_chain, chip_rows(z, xl), :]
     bytes_of(s_recv, l_r.at[t, 0])
     for i in range(2 * NZ - 1):
         acc = acc + s_recv[i].astype(jnp.float32)
@@ -518,12 +520,12 @@
             bytes_of(l_recv.at[0, 0], l_s.at[t, h])
             bytes_of(l_recv.at[0, 0], r_s.at[t, h])
         for own, count in ((True, 3), (False, 4)):
-            @pl.when((xh == h) == own)
+            @pl.when((my_chain == h) == own)
             def _():
                 for t in range(STEPS):
                     bytes_of(g_recv.at[0, 0:count], g_s.at[t, h])
         for own, count in ((True, 7), (False, 8)):
-            @pl.when((zh == h) == own)
+            @pl.when((z_chain == h) == own)
             def _():
                 bytes_of(s_recv.at[0:count], l_s.at[STEPS, h])
 

time: 95.6 us -> 94.5 us (0.988)
  Pallas kernels: 93.6 us -> 92.5 us
    pallas_call x1, Pallas kernels: 93.6 us -> 92.5 us  [per_device(): pl.pallas_call(functools.partial(kernel, scale), out_shape=(pltpu.VMEM((k...]
where the time goes in v7:
time: 94.5 us; the launch traced here: 94.4 us
  Pallas kernels  92.5 us (98%)
  local copies, waits for them, and re-layouts  1.22 us (1%)
    pallas_call x1, Pallas kernels, per_device(): pl.pallas_call(functools.partial(kernel, scale), out_shape=(pltpu.VMEM((k...  92.5 us

profile of v7, /device:TPU:1, one launch (start us, length us, event | category | flops | bytes accessed | tf_op | source)
XLA Modules:
  0.0 94.4 jit_solution(13891494147543154209)
XLA Ops:
  0.6 92.5 %shard_map.68 = (f32[16,640]{1,0:T(8,128)S(1)}, f32[4,1024]{1,0:T(4,128)S(1)}) custom-call(f32[36,1024]{1,0:T(8,128)} %bitcast.7, f32[144,640]{1,0:T(8,128)} %f_hbm.1, f32[5,128]{1,0:T(8,128)} %bitcast.9, f32[16,640]{1,0:T(8,128)} %bitcast.8, s32[1024,128]{1,0:T(8,128)} %lab_hbm.1), custom_call_target="tpu_custom_call" | custom-call | tf_op jit(solution)/shard_map/pallas_call | solution.py:588
  93.2 0.6 copy.9
  93.8 0.6 copy.10

commit v8 on v7

--- a/solution.py
+++ b/solution.py
@@ -45,7 +45,7 @@
     w_own, w_send, w_t,
     part, c_send, c_recv, l_send, l_recv, r_t,
     grad, g_send, g_recv, logits, s_out, s_in, s_own, s_sum, s_recv,
-    eq_s, eq_r, er_s, er_r, ep_s, ep_r,
+    eq_s, eq_r, en_s, er_s, er_r, ep_s, ep_r,
     fx_s, fx_r, fy_s, fy_r,
     w_s, w_r, c_s, c_r, l_s, l_r, r_s, r_r, rc_s, rc_r, g_s, g_r,
     in_s, hello,
@@ -149,9 +149,12 @@
     def send_w(u, dy):
         put(w_send.at[0], w_t.at[0, my_rows, :], w_s.at[0], w_r.at[0, 0], (clip_of(u, dy), feat), False)
 
-    put(e_ref.at[:, lanes_o], e_raw.at[0], eq_s.at[0], eq_r.at[0], partner)
-    put(e_ref.at[:, lanes_c], e_raw.at[1], eq_s.at[1], eq_r.at[1], x_near)
-    put(e_ref.at[:, lanes_o], e_raw.at[2], eq_s.at[2], eq_r.at[2], diag)
+    put(e_ref.at[:, lanes_o], e_raw.at[0], eq_s.at[0, 0], eq_r.at[0, 0], partner)
+    for q in range(2):
+        part_q = slice(q * quarter, (q + 1) * quarter)
+        for i, core, to in ((1, c, x_near), (2, 1 - c, diag)):
+            lanes_q = pl.ds(pl.multiple_of(core * half + q * quarter, quarter), quarter)
+            put(e_ref.at[:, lanes_q], e_raw.at[i, :, part_q], eq_s.at[i, q], eq_r.at[i, q], to)
 
     cut = kc // 3
     mid = kc // 2
@@ -170,19 +173,17 @@
             f_send(direction, 0, k, clip, lo, lo + mid, f_ref.at[lo:lo + mid, :])
     def join(own, oth):
         first = c == 0
-        e_two[0:ke, :] = jnp.where(first, own, oth)
-        e_two[ke:2 * ke, :] = jnp.where(first, oth, own)
-        return e_two[...]
-
-    def e_start(o, xl_):
-        piece = e_piece(z, xl_)
-        put(piece, piece, er_s.at[0, o, 0], er_r.at[0, o, 0], z_up)
-        put(piece, piece, er_s.at[1, o, 0], er_r.at[1, o, 0], z_down)
-        put(piece, piece, ep_s.at[o, 0], ep_r.at[0], partner)
-
-    bytes_of(e_raw.at[0], eq_r.at[0])
+        lanes = own.shape[1]
+        e_two[0:ke, 0:lanes] = jnp.where(first, own, oth)
+        e_two[ke:2 * ke, 0:lanes] = jnp.where(first, oth, own)
+        return e_two[:, 0:lanes]
+
+    bytes_of(e_raw.at[0], eq_r.at[0, 0])
     e_all[e_rows(z, xl), lanes_c] = join(e_ref[:, lanes_c], e_raw[0])
-    e_start(0, xl)
+    own_piece = e_piece(z, xl)
+    put(own_piece, own_piece, er_s.at[0, 0, 0], er_r.at[0, 0, 0], z_up)
+    put(own_piece, own_piece, er_s.at[1, 0, 0], er_r.at[1, 0, 0], z_down)
+    put(own_piece, own_piece, ep_s.at[0, 0], ep_r.at[0], partner)
 
     greeted(0)
     greet(1)
@@ -206,10 +207,17 @@
         for n in range(nn // 128):
             ang[128 * b:128 * b + 128, 128 * n:128 * n + 128] = column
 
-    bytes_of(e_raw.at[1], eq_r.at[1])
-    bytes_of(e_raw.at[2], eq_r.at[2])
-    e_all[e_rows(z, 1 - xl), lanes_c] = join(e_raw[1], e_raw[2])
-    e_start(1, 1 - xl)
+    near_piece = e_piece(z, 1 - xl)
+    for q in range(2):
+        part_q = slice(q * quarter, (q + 1) * quarter)
+        bytes_of(e_raw.at[1, :, part_q], eq_r.at[1, q])
+        bytes_of(e_raw.at[2, :, part_q], eq_r.at[2, q])
+        lanes_q = pl.ds(pl.multiple_of(c * half + q * quarter, quarter), quarter)
+        e_all[e_rows(z, 1 - xl), lanes_q] = join(e_raw[1, :, part_q], e_raw[2, :, part_q])
+        near_q = e_far_piece(z, 1 - xl, q)
+        put(near_q, near_q, en_s.at[0, q], er_r.at[0, 1, 0], z_up)
+        put(near_q, near_q, en_s.at[1, q], er_r.at[1, 1, 0], z_down)
+    put(near_piece, near_piece, ep_s.at[1, 0], ep_r.at[0], partner)
 
     def e_step(direction, o, s):
         dz = (NZ - s) if direction == 0 else s
@@ -326,7 +334,6 @@
     e_other(6)
     e_step(0, 0, 3)
     e_step(1, 0, 3)
-    products(2, 0, 2)
     f_wait(0, 1, 0, clip_of(1, 3), 0, cut)
     f_wait(0, 1, 1, clip_of(1, 3), cut, mid)
     f_send(0, 1, 3, clip_of(1, 3), 0, mid)
@@ -336,7 +343,7 @@
     greeted(2)
     for u, dy in clip_offsets:
         send_w(u, dy)
-    products(2, 2, 6)
+    products(2, 0, 8)
     e_step(0, 1, 3)
     e_step(1, 1, 3)
     f_wait(0, 1, 2, clip_of(1, 3), mid, kc)
@@ -579,7 +586,7 @@
         pltpu.VMEM((2, 128, quarter), f32),
         pltpu.VMEM((2, 128, quarter), b16),
         pltpu.VMEM((2 * NZ - 1, 16, quarter), b16),
-        dma((3,)), dma((3,)), dma((2, 2, 4)), dma((2, 2, 4)), dma((2, NZ + 1)), dma((NZ,)),
+        dma((3, 2)), dma((3, 2)), dma((2, 2)), dma((2, 2, 4)), dma((2, 2, 4)), dma((2, NZ + 1)), dma((NZ,)),
         dma((4,)), dma((4,)), dma((2, 2, 4)), dma((2, 2, 4)),
         dma((steps,)), dma((steps, 2)), dma((steps, 2)), dma((steps, 2)), dma((steps, 2)), dma((steps, 2)),
         dma((STEPS, 2)), dma((STEPS, 2)), dma((STEPS, 2)), dma((STEPS, 2)), dma((STEPS, 2)), dma((STEPS,)),

time: 94.5 us -> 94.2 us (level)
  no operation moved by 1% of the time
where the time goes in v8:
time: 94.2 us; the launch traced here: 94.1 us
  Pallas kernels  92.2 us (98%)
  local copies, waits for them, and re-layouts  1.22 us (1%)
    pallas_call x1, Pallas kernels, per_device(): pl.pallas_call(functools.partial(kernel, scale), out_shape=(pltpu.VMEM((k...  92.2 us

profile of v8, /device:TPU:1, one launch (start us, length us, event | category | flops | bytes accessed | tf_op | source)
XLA Modules:
  0.0 94.1 jit_solution(16095116397975453996)
XLA Ops:
  0.6 92.2 %shard_map.68 = (f32[16,640]{1,0:T(8,128)S(1)}, f32[4,1024]{1,0:T(4,128)S(1)}) custom-call(f32[36,1024]{1,0:T(8,128)} %bitcast.7, f32[144,640]{1,0:T(8,128)} %f_hbm.1, f32[5,128]{1,0:T(8,128)} %bitcast.9, f32[16,640]{1,0:T(8,128)} %bitcast.8, s32[1024,128]{1,0:T(8,128)} %lab_hbm.1), custom_call_target="tpu_custom_call" | custom-call | tf_op jit(solution)/shard_map/pallas_call | solution.py:595
  92.8 0.6 copy.9
  93.5 0.6 copy.10

commit v9 on v8

--- a/solution.py
+++ b/solution.py
@@ -365,11 +365,12 @@
     f_wait(0, 1, 3, clip_of(1, 2), 0, mid)
     f_wait(1, 1, 3, clip_of(1, 2), mid, kc)
     f_prep(1, 2)
+    ang[...] = ang[...] + dot(f3[beside], e3[beside])
     e_other(4)
 
     for n in range(nn // 256):
         cols = slice(256 * n, 256 * n + 256)
-        x = ang[:, cols] + dot(f3[beside], e3[beside, :, cols]) + dot(f3[far], e3[far, :, cols])
+        x = ang[:, cols] + dot(f3[far], e3[far, :, cols])
         phi[:, cols] = scaled_cos_of_twice(x, scale).astype(jnp.bfloat16)
 
     hk = w_t.shape[1] // 2

time: 94.2 us -> 94.2 us (level)
  no operation moved by 1% of the time
where the time goes in v9:
time: 94.2 us; the launch traced here: 94.1 us
  Pallas kernels  92.3 us (98%)
  local copies, waits for them, and re-layouts  1.22 us (1%)
    pallas_call x1, Pallas kernels, per_device(): pl.pallas_call(functools.partial(kernel, scale), out_shape=(pltpu.VMEM((k...  92.3 us

profile of v9, /device:TPU:1, one launch (start us, length us, event | category | flops | bytes accessed | tf_op | source)
XLA Modules:
  0.0 94.1 jit_solution(3704880936188390815)
XLA Ops:
  0.6 92.3 %shard_map.68 = (f32[16,640]{1,0:T(8,128)S(1)}, f32[4,1024]{1,0:T(4,128)S(1)}) custom-call(f32[36,1024]{1,0:T(8,128)} %bitcast.7, f32[144,640]{1,0:T(8,128)} %f_hbm.1, f32[5,128]{1,0:T(8,128)} %bitcast.9, f32[16,640]{1,0:T(8,128)} %bitcast.8, s32[1024,128]{1,0:T(8,128)} %lab_hbm.1), custom_call_target="tpu_custom_call" | custom-call | tf_op jit(solution)/shard_map/pallas_call | solution.py:596
  92.9 0.6 copy.9
  93.5 0.6 copy.10

commit v10 on v9

--- a/solution.py
+++ b/solution.py
@@ -457,7 +457,7 @@
 
             for yo in (2 * h, 2 * h + 1):
                 send_g(1, yo)
-
+            for yo in (2 * h, 2 * h + 1):
                 @pl.when(yo != y)
                 def _():
                     send_g(0, yo)
@@ -508,7 +508,7 @@
 
         for pz in (2 * h, 2 * h + 1, NY + 2 * h, NY + 2 * h + 1):
             send_s(pz, 1)
-
+        for pz in (2 * h, 2 * h + 1, NY + 2 * h, NY + 2 * h + 1):
             @pl.when(pz != z)
             def _():
                 send_s(pz, 0)

time: 94.2 us -> 94.2 us (level)
  no operation moved by 1% of the time
where the time goes in v10:
time: 94.2 us; the launch traced here: 94.1 us
  Pallas kernels  92.3 us (98%)
  local copies, waits for them, and re-layouts  1.22 us (1%)
    pallas_call x1, Pallas kernels, per_device(): pl.pallas_call(functools.partial(kernel, scale), out_shape=(pltpu.VMEM((k...  92.3 us

profile of v10, /device:TPU:1, one launch (start us, length us, event | category | flops | bytes accessed | tf_op | source)
XLA Modules:
  0.0 94.1 jit_solution(6306183435088463370)
XLA Ops:
  0.6 92.3 %shard_map.68 = (f32[16,640]{1,0:T(8,128)S(1)}, f32[4,1024]{1,0:T(4,128)S(1)}) custom-call(f32[36,1024]{1,0:T(8,128)} %bitcast.7, f32[144,640]{1,0:T(8,128)} %f_hbm.1, f32[5,128]{1,0:T(8,128)} %bitcast.9, f32[16,640]{1,0:T(8,128)} %bitcast.8, s32[1024,128]{1,0:T(8,128)} %lab_hbm.1), custom_call_target="tpu_custom_call" | custom-call | tf_op jit(solution)/shard_map/pallas_call | solution.py:596
  92.9 0.6 copy.9
  93.5 0.6 copy.10
